TPU v7x, 32 devices: a whole 2x2x4 slice. The times are simulated.
32 devices in a mesh: ctx: 8 (over y, x, core), head: 4 (over z).
Axes of the slice: x: 2, y: 2, z: 4, core: 2. Of those that a mesh axis runs over, the one named last changes fastest.
Arguments:
- tokens_x: bfloat16 [4096, 8192], P('ctx', 'head'), may hold values from -121 to 121
- raw_dt: float32 [128, 4096], P('head', 'ctx'), may hold values from -4 to 4
- in_b: bfloat16 [4096, 128], P('ctx'), may hold values from -0.5 to 0.5
- in_c: bfloat16 [4096, 128], P('ctx'), may hold values from -0.5 to 0.5
- decay_rate: float32 [128], P('head'), may hold values from 4.8828125e-06 to 2
- skip_gain: float32 [128], P('head'), may hold values from 0.5 to 1.5
- step_bias: float32 [128], P('head'), may hold values from -5 to -3
- grad_y: bfloat16 [4096, 8192], P('ctx', 'head'), may hold values from -121 to 121
Outputs:
- grad_x: bfloat16 [4096, 8192], P('ctx', 'head')
- grad_raw_dt: float32 [128, 4096], P('head', 'ctx')
- grad_b: float32 [4096, 128], P('ctx')
- grad_c: float32 [4096, 128], P('ctx')
- grad_rate: float32 [128], P('head')
- grad_skip: float32 [128], P('head')
- grad_bias: float32 [128], P('head')
All inputs are finite; a program needn't handle non-finite values.
Results may differ from a plain program's by a relative error of at most 0.001.
Values sent between devices are 32-bit elements; how exact they have to be, the bound alone decides.
A program may use at most 128 MiB of HBM per device.

v0:
```python
import functools
import types

import jax
import jax.numpy as jnp
from jax import lax
from jax.experimental import pallas as pl
from jax.experimental.pallas import tpu as pltpu
from jax.sharding import PartitionSpec as P

CHUNK = 128
GROUP = 8
F32 = jnp.float32
BF16 = jnp.bfloat16
HIGH = lax.Precision.HIGHEST
NT = (((1,), (1,)), ((), ()))
MESH = pl.DeviceIdType.MESH


def mm(a, b):
    return jnp.dot(a, b, preferred_element_type=F32)


def mm_nt(a, b):
    return lax.dot_general(a, b, NT, preferred_element_type=F32)


def split(a):
    high = a.astype(BF16)
    return high, (a - high.astype(F32)).astype(BF16)


def twice(a, axis):
    return jnp.concatenate([a, a], axis=axis)


def softplus(v):
    return jnp.maximum(v, 0.0) + jnp.log1p(jnp.exp(-jnp.abs(v)))


def lanes(column, width=CHUNK):
    return jnp.broadcast_to(column, (column.shape[0], width))


def per_head(rows, matrix):
    heads = rows.shape[0]
    shaped = matrix.reshape(heads, matrix.shape[0] // heads, matrix.shape[1])
    return (shaped * rows[:, None, :]).reshape(matrix.shape)


def head_sums(matrix, heads):
    return jnp.sum(matrix.reshape(heads, matrix.shape[0] // heads, matrix.shape[1]), axis=1)


def pair_blocks(first, second):
    zero = jnp.zeros_like(first)
    return jnp.concatenate(
        [jnp.concatenate([first, zero], axis=1), jnp.concatenate([zero, second], axis=1)], axis=0
    )


def triangle(lower):
    row = lax.broadcasted_iota(jnp.int32, (CHUNK, CHUNK), 0)
    col = lax.broadcasted_iota(jnp.int32, (CHUNK, CHUNK), 1)
    return (row >= col) if lower else (row <= col)


def eye(n):
    row = lax.broadcasted_iota(jnp.int32, (n, n), 0)
    col = lax.broadcasted_iota(jnp.int32, (n, n), 1)
    return row == col


def column_of(row):
    n = row.shape[1]
    return jnp.sum(jnp.where(eye(n), jnp.broadcast_to(row, (n, n)), 0.0), axis=1, keepdims=True)


def row_of(column):
    n = column.shape[0]
    return jnp.sum(jnp.where(eye(n), jnp.broadcast_to(column, (n, n)), 0.0), axis=0, keepdims=True)


def span_of(c):
    return slice(c * CHUNK, (c + 1) * CHUNK)


def inputs_and_outputs():
    return ("x_hbm", "g_hbm", "raw", "bias", "rate", "skip", "b", "c",
            "gx_hbm", "graw", "gb", "gc", "grate", "gskip", "gbias")


def scratch_of(heads, tokens, size, state, peers):
    groups, chunks, chips = heads // GROUP, tokens // CHUNK, peers // 2
    wide, half = GROUP * size, size // 2
    vmem = pltpu.VMEM
    dma = pltpu.SemaphoreType.DMA
    halves = (groups, GROUP, half, state)
    return dict(
        x=vmem((groups, tokens, wide), BF16),
        g=vmem((groups, tokens, wide), BF16),
        xt=vmem((groups, wide, tokens), BF16),
        gt=vmem((groups, wide, tokens), BF16),
        dt=vmem((heads, tokens), F32),
        cum=vmem((heads, tokens), F32),
        weight=vmem((heads, tokens), F32),
        reach=vmem((heads, tokens), F32),
        step=vmem((chunks, heads, CHUNK), F32),
        before=vmem((chunks + 1, heads, CHUNK), F32),
        after=vmem((chunks + 1, heads, CHUNK), F32),
        s=vmem((groups, chunks, wide, state), F32),
        r=vmem((groups, chunks, wide, state), F32),
        total=vmem((2, groups, GROUP, size, state), F32),
        ends=vmem((peers, heads, CHUNK), F32),
        coef=vmem((2, chips, heads, CHUNK), F32),
        pair_in=vmem((2,) + halves, F32),
        agg=vmem((2,) + halves, F32),
        chip_in=vmem((chips,) + halves, F32),
        give=vmem((2,) + halves, F32),
        state_in=vmem((2, groups, GROUP, size, state), F32),
        dxt=vmem((groups, chunks, wide, CHUNK), F32),
        row=vmem((groups, chunks, GROUP, CHUNK), F32),
        col=vmem((groups, chunks, GROUP, CHUNK), F32),
        cross=vmem((groups, GROUP, CHUNK), F32),
        dg=vmem((chunks, CHUNK, CHUNK), F32),
        parts=vmem((groups, chunks, 4, wide, state), BF16),
        gx=vmem((groups, chunks, CHUNK, wide), BF16),
        zown=vmem((chunks, 2, CHUNK, state), F32),
        zsum=vmem((chunks, 2, CHUNK, state), F32),
        zin=vmem((2, chunks, 2, CHUNK, state), F32),
        ztot=vmem((chunks, 2, CHUNK, state), F32),
        params=vmem((heads, CHUNK), F32),
        params_in=vmem((peers, heads, CHUNK), F32),
        load_sem=dma((2, groups)),
        end_send=dma((peers,)),
        end_recv=dma((peers,)),
        pair_send=dma((2, groups)),
        pair_recv=dma((2, groups)),
        chip_send=dma((chips, groups)),
        chip_recv=dma((chips, groups)),
        back_send=dma((2, groups)),
        back_recv=dma((2, groups)),
        in_send=dma((chunks, 2)),
        out_send=dma((chunks, 2)),
        z_recv=dma((2, chunks, 2)),
        param_send=dma((peers,)),
        param_recv=dma((peers,)),
        gx_sem=dma((groups, chunks)),
    )


def kernel(names, peers, line, *refs):
    k = types.SimpleNamespace(**dict(zip(names, refs)))
    heads, tokens = k.raw.shape
    state = k.b.shape[1]
    groups, chunks, chips = heads // GROUP, tokens // CHUNK, peers // 2
    wide = k.x.shape[2]
    size = wide // GROUP
    half = size // 2
    me, zpos = lax.axis_index("ctx"), lax.axis_index("head")
    odd, chip = me % 2, me // 2
    is_odd = odd == 1
    mate = me + 1 - 2 * odd

    left = zpos < line // 2
    inner = jnp.where(left, zpos + 1, zpos - 1)
    outer = jnp.where(left, zpos - 1, zpos + 1)
    has_outer = jnp.logical_and(zpos > 0, zpos < line - 1)
    is_mid = jnp.logical_or(zpos == line // 2 - 1, zpos == line // 2)
    in_slot = jnp.where(is_mid, 1, 0)

    barrier = pltpu.get_barrier_semaphore()
    for d in range(1, peers):
        pl.semaphore_signal(barrier, inc=1, device_id={"ctx": (me + d) % peers}, device_id_type=MESH)
    pl.semaphore_signal(barrier, inc=1, device_id={"head": inner}, device_id_type=MESH)

    @pl.when(has_outer)
    def _():
        pl.semaphore_signal(barrier, inc=1, device_id={"head": outer}, device_id_type=MESH)

    def load(i, group):
        src, dst = ((k.x_hbm, k.x), (k.g_hbm, k.g))[i]
        at = pl.ds(pl.multiple_of(group * wide, wide), wide)
        return pltpu.make_async_copy(src.at[:, at], dst.at[group], k.load_sem.at[i, group])

    for group in range(groups):
        load(0, group).start()
        load(1, group).start()

    dt = softplus(k.raw[...] + column_of(k.bias[...]))
    k.dt[...] = dt
    rate = column_of(k.rate[...])
    log_decay = -rate * dt
    ones = triangle(False).astype(F32)
    cums = [jnp.dot(log_decay[:, span_of(c)], ones, precision=HIGH) for c in range(chunks)]
    ends = [lanes(cum[:, CHUNK - 1:]) for cum in cums]
    before, after = jnp.zeros_like(ends[0]), jnp.zeros_like(ends[0])
    for c in range(chunks):
        k.before[c] = jnp.exp(before)
        before = before + ends[c]
        k.after[chunks - c] = jnp.exp(after)
        after = after + ends[chunks - 1 - c]
    k.before[chunks] = jnp.exp(before)
    k.after[0] = jnp.exp(after)
    k.ends[me] = before
    for c in range(chunks):
        k.cum[:, span_of(c)] = cums[c]
        k.reach[:, span_of(c)] = jnp.exp(cums[c])
        k.weight[:, span_of(c)] = jnp.exp(ends[c] - cums[c]) * dt[:, span_of(c)]
        k.step[c] = jnp.exp(ends[c])
    k.dg[...] = jnp.zeros_like(k.dg)

    pl.semaphore_wait(barrier, peers + jnp.where(has_outer, 1, 0))

    def send_end(d):
        return pltpu.make_async_remote_copy(
            src_ref=k.ends.at[me], dst_ref=k.ends.at[me],
            send_sem=k.end_send.at[d], recv_sem=k.end_recv.at[d],
            device_id={"ctx": (me + d) % peers}, device_id_type=MESH)

    def recv_end(d):
        place = (me - d + peers) % peers
        return pltpu.make_async_remote_copy(
            src_ref=k.ends.at[place], dst_ref=k.ends.at[place],
            send_sem=k.end_send.at[d], recv_sem=k.end_recv.at[d],
            device_id={"ctx": place}, device_id_type=MESH)

    for d in range(1, peers):
        send_end(d).start()

    mine = pl.ds(pl.multiple_of(odd * half, half), half)
    theirs = pl.ds(pl.multiple_of((1 - odd) * half, half), half)

    def pair_copy(i, group):
        return pltpu.make_async_remote_copy(
            src_ref=k.total.at[i, group, :, theirs, :], dst_ref=k.pair_in.at[i, group],
            send_sem=k.pair_send.at[i, group], recv_sem=k.pair_recv.at[i, group],
            device_id={"ctx": mate}, device_id_type=MESH)

    def chip_copy(step, group):
        what = jnp.where(chip + step < chips, 0, 1)
        return pltpu.make_async_remote_copy(
            src_ref=k.agg.at[what, group], dst_ref=k.chip_in.at[step, group],
            send_sem=k.chip_send.at[step, group], recv_sem=k.chip_recv.at[step, group],
            device_id={"ctx": (me + 2 * step) % peers}, device_id_type=MESH)

    def back_copy(i, group):
        return pltpu.make_async_remote_copy(
            src_ref=k.give.at[i, group], dst_ref=k.state_in.at[i, group, :, mine, :],
            send_sem=k.back_send.at[i, group], recv_sem=k.back_recv.at[i, group],
            device_id={"ctx": mate}, device_id_type=MESH)

    def back_arrival(i, group):
        return pltpu.make_async_remote_copy(
            src_ref=k.give.at[i, group], dst_ref=k.state_in.at[i, group, :, theirs, :],
            send_sem=k.back_send.at[i, group], recv_sem=k.back_recv.at[i, group],
            device_id={"ctx": mate}, device_id_type=MESH)

    def rows_of(group):
        return pl.ds(pl.multiple_of(group * GROUP, GROUP), GROUP)

    def states(group):
        at_rows = rows_of(group)
        load(0, group).wait()
        load(1, group).wait()
        k.xt[group] = k.x[group].T
        k.gt[group] = k.g[group].T
        value = None
        for c in range(chunks):
            at = span_of(c)
            k.s[group, c] = jnp.zeros((wide, state), F32) if value is None else value
            high, low = split(per_head(k.weight[at_rows, at], k.xt[group, :, at].astype(F32)))
            added = mm(jnp.concatenate([high, low], axis=1), twice(k.b[at, :], 0))
            value = added if value is None else per_head(k.step[c, at_rows], value) + added
        k.total[0, group] = value.reshape(GROUP, size, state)
        value = None
        for c in reversed(range(chunks)):
            at = span_of(c)
            k.r[group, c] = jnp.zeros((wide, state), F32) if value is None else value
            high, low = split(per_head(k.reach[at_rows, at], k.gt[group, :, at].astype(F32)))
            added = mm(jnp.concatenate([high, low], axis=1), twice(k.c[at, :], 0))
            value = added if value is None else per_head(k.step[c, at_rows], value) + added
        k.total[1, group] = value.reshape(GROUP, size, state)

    def make_coefs():
        for d in range(1, peers):
            recv_end(d).wait_recv()
        s_log = jnp.zeros((heads, CHUNK), F32)
        r_log = jnp.zeros((heads, CHUNK), F32)
        for step in range(1, chips):
            k.coef[0, step] = jnp.where(chip >= step, jnp.exp(s_log), 0.0)
            k.coef[1, step] = jnp.where(chip + step < chips, jnp.exp(r_log), 0.0)
            low = (chip - step + chips) % chips
            high = (chip + step) % chips
            s_log = s_log + (k.ends[2 * low] + k.ends[2 * low + 1])
            r_log = r_log + (k.ends[2 * high] + k.ends[2 * high + 1])

    def own_and_mate(group):
        at_rows = rows_of(group)
        return jnp.exp(k.ends[me, at_rows]), jnp.exp(k.ends[mate, at_rows])

    def scaled(coef, block):
        return coef[:, None, :] * block

    def combine(group):
        own_e, mate_e = own_and_mate(group)
        one = jnp.ones_like(own_e)
        pair_copy(0, group).wait_recv()
        k.agg[0, group] = (scaled(jnp.where(is_odd, one, mate_e), k.total[0, group, :, mine, :])
                           + scaled(jnp.where(is_odd, own_e, one), k.pair_in[0, group]))
        pair_copy(1, group).wait_recv()
        k.agg[1, group] = (scaled(jnp.where(is_odd, mate_e, one), k.total[1, group, :, mine, :])
                           + scaled(jnp.where(is_odd, one, own_e), k.pair_in[1, group]))
        for step in range(1, chips):
            chip_copy(step, group).start()

    def finalize(group):
        at_rows = rows_of(group)
        own_e, mate_e = own_and_mate(group)
        one, zero = jnp.ones_like(own_e), jnp.zeros_like(own_e)
        s_pre = jnp.zeros((GROUP, half, state), F32)
        r_pre = jnp.zeros((GROUP, half, state), F32)
        for step in range(1, chips):
            chip_copy(step, group).wait_recv()
            got = k.chip_in[step, group]
            s_pre = s_pre + scaled(k.coef[0, step, at_rows], got)
            r_pre = r_pre + scaled(k.coef[1, chips - step, at_rows], got)
        k.give[0, group] = (scaled(jnp.where(is_odd, one, own_e), s_pre)
                            + scaled(jnp.where(is_odd, zero, one), k.total[0, group, :, mine, :]))
        k.give[1, group] = (scaled(jnp.where(is_odd, own_e, one), r_pre)
                            + scaled(jnp.where(is_odd, one, zero), k.total[1, group, :, mine, :]))
        k.state_in[0, group, :, mine, :] = (scaled(jnp.where(is_odd, mate_e, one), s_pre)
                                            + scaled(jnp.where(is_odd, one, zero), k.pair_in[0, group]))
        back_copy(0, group).start()
        k.state_in[1, group, :, mine, :] = (scaled(jnp.where(is_odd, one, mate_e), r_pre)
                                            + scaled(jnp.where(is_odd, zero, one), k.pair_in[1, group]))
        back_copy(1, group).start()

    def first_step(group, carry):
        states(group)
        pair_copy(0, group).start()
        pair_copy(1, group).start()

        @pl.when(group == 0)
        def _():
            make_coefs()

        @pl.when(group > 0)
        def _():
            combine(group - 1)

        return carry

    lax.fori_loop(0, groups, first_step, 0)
    combine(groups - 1)

    causal = triangle(False)

    def within(group):
        def one_chunk(c, carry):
            at = pl.ds(pl.multiple_of(c * CHUNK, CHUNK), CHUNK)
            scores = mm_nt(k.b[at, :], k.c[at, :])
            cum = k.cum[rows_of(group), at]
            shifted = (cum - jnp.log(k.dt[rows_of(group), at])).T
            total = jnp.zeros((CHUNK, CHUNK), F32)
            rows, cols = [], []
            for pair in range(GROUP // 2):
                x_pair = k.x[group, at, pair * 2 * size:(pair + 1) * 2 * size]
                places = [slice((2 * pair + j) * size, (2 * pair + j + 1) * size) for j in range(2)]
                products = mm(x_pair, pair_blocks(k.gt[group, places[0], at], k.gt[group, places[1], at]))
                for j in range(2):
                    h = 2 * pair + j
                    gap = cum[h:h + 1, :] - shifted[:, h:h + 1]
                    decay = jnp.exp(jnp.where(causal, gap, -1e30))
                    both = products[:, j * CHUNK:(j + 1) * CHUNK] * decay
                    total = total + both
                    rows.append(jnp.sum(both * scores, axis=0, keepdims=True))
                    high, low = split(decay * scores)
                    dx_h = mm_nt(twice(k.gt[group, places[j], at], 1), jnp.concatenate([high, low], axis=1))
                    k.dxt[group, c, places[j], :] = dx_h
                    x_h = k.xt[group, places[j], at]
                    cols.append(jnp.sum(dx_h * x_h.astype(F32), axis=0, keepdims=True))
            k.row[group, c] = jnp.concatenate(rows, axis=0)
            k.col[group, c] = jnp.concatenate(cols, axis=0)
            k.dg[c] += total
            return carry

        lax.fori_loop(0, chunks, one_chunk, 0)

    def second_step(group, carry):
        within(group)

        @pl.when(group > 0)
        def _():
            finalize(group - 1)

        return carry

    lax.fori_loop(0, groups, second_step, 0)
    finalize(groups - 1)

    def inward(c, i, source):
        return pltpu.make_async_remote_copy(
            src_ref=source.at[c, i], dst_ref=k.zin.at[in_slot, c, i],
            send_sem=k.in_send.at[c, i], recv_sem=k.z_recv.at[in_slot, c, i],
            device_id={"head": inner}, device_id_type=MESH)

    def outward(c, i):
        return pltpu.make_async_remote_copy(
            src_ref=k.ztot.at[c, i], dst_ref=k.zin.at[1, c, i],
            send_sem=k.out_send.at[c, i], recv_sem=k.z_recv.at[1, c, i],
            device_id={"head": outer}, device_id_type=MESH)

    def arrival(slot, c, i):
        return pltpu.make_async_remote_copy(
            src_ref=k.ztot.at[c, i], dst_ref=k.zin.at[slot, c, i],
            send_sem=k.out_send.at[c, i], recv_sem=k.z_recv.at[slot, c, i],
            device_id={"head": inner}, device_id_type=MESH)

    def publish(c):
        @pl.when(jnp.logical_not(has_outer))
        def _():
            for i in range(2):
                inward(c, i, k.zown).start()

    def relay(c):
        @pl.when(has_outer)
        def _():
            for i in range(2):
                arrival(0, c, i).wait_recv()
                k.zsum[c, i] = k.zown[c, i] + k.zin[0, c, i]
                inward(c, i, k.zsum).start()

    def settle(c):
        for i in range(2):
            arrival(1, c, i).wait_recv()

            @pl.when(jnp.logical_and(is_mid, has_outer))
            def _():
                k.ztot[c, i] = k.zsum[c, i] + k.zin[1, c, i]

            @pl.when(jnp.logical_and(is_mid, jnp.logical_not(has_outer)))
            def _():
                k.ztot[c, i] = k.zown[c, i] + k.zin[1, c, i]

            @pl.when(jnp.logical_not(is_mid))
            def _():
                k.ztot[c, i] = k.zin[1, c, i]

            @pl.when(has_outer)
            def _():
                outward(c, i).start()

            (k.gb, k.gc)[i][span_of(c), :] = k.ztot[c, i]

    def projections(c):
        at = span_of(c)
        b, cc = k.b[at, :], k.c[at, :]
        high, low = split(k.dg[c])
        k.zown[c, 0] = mm(jnp.concatenate([high, low], axis=1), twice(cc, 0))
        high, low = split(k.dg[c].T)
        k.zown[c, 1] = mm(jnp.concatenate([high, low], axis=1), twice(b, 0))

        def one_group(group, carry):
            if c == 0:
                for i in range(2):
                    back_arrival(i, group).wait_recv()
            at_rows = rows_of(group)
            s_in = k.state_in[0, group].reshape(wide, state)
            r_in = k.state_in[1, group].reshape(wide, state)
            for i, (coef, incoming, local, scale, ref) in enumerate((
                    (k.before[c, at_rows], s_in, k.s, k.reach, k.g),
                    (k.after[c + 1, at_rows], r_in, k.r, k.weight, k.x))):
                high, low = split(per_head(coef, incoming) + local[group, c])
                k.parts[group, c, 2 * i] = high
                k.parts[group, c, 2 * i + 1] = low
                column = scale[at_rows, at].T
                total = jnp.zeros((CHUNK, state), F32)
                for pair in range(GROUP // 2):
                    wide_at = slice(pair * 2 * size, (pair + 1) * 2 * size)
                    one = slice(2 * pair * size, (2 * pair + 1) * size)
                    two = slice((2 * pair + 1) * size, (2 * pair + 2) * size)
                    both = mm(twice(ref[group, at, wide_at], 1),
                              jnp.concatenate([pair_blocks(high[one], high[two]),
                                               pair_blocks(low[one], low[two])], axis=0))
                    for j in range(2):
                        h = 2 * pair + j
                        total = total + both[:, j * state:(j + 1) * state] * column[:, h:h + 1]
                k.zown[c, 1 - i] += total
            return carry

        lax.fori_loop(0, groups, one_group, 0)

    def inputs_step(c):
        at = span_of(c)
        bb, cc = twice(k.b[at, :], 1), twice(k.c[at, :], 1)

        def one_group(group, carry):
            at_rows = rows_of(group)
            weight, reach = k.weight[at_rows, at], k.reach[at_rows, at]
            xt, gt = k.xt[group, :, at].astype(F32), k.gt[group, :, at].astype(F32)
            parts = [k.parts[group, c, i] for i in range(4)]
            y = mm_nt(jnp.concatenate(parts[:2], axis=1), cc)
            k.row[group, c] += head_sums(y * gt, GROUP) * reach
            dx = per_head(weight, mm_nt(jnp.concatenate(parts[2:], axis=1), bb))
            k.col[group, c] += head_sums(dx * xt, GROUP)
            product = head_sums(xt * gt, GROUP)
            k.cross[group] = product if c == 0 else k.cross[group] + product
            skip = lanes(column_of(k.skip[...]))
            k.params[...] = skip
            dx = dx + k.dxt[group, c] + per_head(k.params[at_rows], gt)
            k.gx[group, c] = dx.astype(BF16).T
            gx_copy(group, c).start()
            return carry

        lax.fori_loop(0, groups, one_group, 0)

    def gx_copy(group, c):
        at = pl.ds(pl.multiple_of(group * wide, wide), wide)
        return pltpu.make_async_copy(k.gx.at[group, c], k.gx_hbm.at[span_of(c), at], k.gx_sem.at[group, c])

    for c in range(chunks):
        projections(c)
        publish(c)
    for c in range(chunks):
        inputs_step(c)
        relay(c)
        if c > 0:
            settle(c - 1)

    beyond = []
    for group in range(groups):
        at_rows = rows_of(group)
        last = k.total[0, group].reshape(wide, state) + per_head(
            k.before[chunks, at_rows], k.state_in[0, group].reshape(wide, state))
        beyond.append(jnp.sum(head_sums(last * k.state_in[1, group].reshape(wide, state), GROUP),
                              axis=1, keepdims=True))
    beyond = lanes(jnp.concatenate(beyond, axis=0))
    suffix = triangle(True).astype(F32)
    bias = column_of(k.bias[...])
    g_rate = jnp.zeros((heads, 1), F32)
    g_bias = jnp.zeros((heads, 1), F32)
    for c in reversed(range(chunks)):
        at = span_of(c)
        row = jnp.concatenate([k.row[group, c] for group in range(groups)], axis=0)
        col = jnp.concatenate([k.col[group, c] for group in range(groups)], axis=0)
        change = row - col
        d_log = jnp.dot(change, suffix, precision=HIGH) + beyond
        beyond = beyond + lanes(jnp.sum(change, axis=1, keepdims=True))
        dt = k.dt[:, at]
        g_dt = col / dt - rate * d_log
        g_raw = g_dt / (1.0 + jnp.exp(-(k.raw[:, at] + bias)))
        k.graw[:, at] = g_raw
        g_rate = g_rate - jnp.sum(dt * d_log, axis=1, keepdims=True)
        g_bias = g_bias + jnp.sum(g_raw, axis=1, keepdims=True)
    cross = jnp.concatenate([k.cross[group] for group in range(groups)], axis=0)
    g_skip = jnp.sum(cross, axis=1, keepdims=True)
    lane = lax.broadcasted_iota(jnp.int32, (heads, CHUNK), 1)
    k.params_in[me] = jnp.where(lane == 0, g_rate, jnp.where(lane == 1, g_skip, g_bias))

    def send_params(d):
        return pltpu.make_async_remote_copy(
            src_ref=k.params_in.at[me], dst_ref=k.params_in.at[me],
            send_sem=k.param_send.at[d], recv_sem=k.param_recv.at[d],
            device_id={"ctx": (me + d) % peers}, device_id_type=MESH)

    def recv_params(d):
        place = (me - d + peers) % peers
        return pltpu.make_async_remote_copy(
            src_ref=k.params_in.at[place], dst_ref=k.params_in.at[place],
            send_sem=k.param_send.at[d], recv_sem=k.param_recv.at[d],
            device_id={"ctx": place}, device_id_type=MESH)

    for d in range(1, peers):
        send_params(d).start()
    settle(chunks - 1)
    for d in range(1, peers):
        recv_params(d).wait_recv()
    total = k.params_in[0]
    for d in range(1, peers):
        total = total + k.params_in[d]
    k.grate[...] = row_of(total[:, 0:1])
    k.gskip[...] = row_of(total[:, 1:2])
    k.gbias[...] = row_of(total[:, 2:3])

    for group in range(groups):
        for c in range(chunks):
            gx_copy(group, c).wait()
        for i in range(2):
            pair_copy(i, group).wait_send()
            back_copy(i, group).wait_send()
        for step in range(1, chips):
            chip_copy(step, group).wait_send()
    for c in range(chunks):
        for i in range(2):
            inward(c, i, k.zsum).wait_send()

            @pl.when(has_outer)
            def _():
                outward(c, i).wait_send()
    for d in range(1, peers):
        send_end(d).wait_send()
        send_params(d).wait_send()


def on_device(peers, line, tokens_x, raw_dt, in_b, in_c, decay_rate, skip_gain, step_bias, grad_y):
    heads, tokens = raw_dt.shape
    width = tokens_x.shape[1]
    size = width // heads
    state = in_b.shape[1]
    scratch = scratch_of(heads, tokens, size, state, peers)
    names = inputs_and_outputs() + tuple(scratch)

    def shape(*dims, dtype=F32):
        return jax.ShapeDtypeStruct(dims, dtype)

    hbm, vmem = pl.BlockSpec(memory_space=pl.ANY), pl.BlockSpec(memory_space=pltpu.VMEM)
    gx, graw, gb, gc, grate, gskip, gbias = pl.pallas_call(
        functools.partial(kernel, names, peers, line),
        in_specs=[hbm, hbm] + [vmem] * 6,
        out_specs=[hbm] + [vmem] * 6,
        out_shape=[shape(tokens, width, dtype=BF16), shape(heads, tokens), shape(tokens, state),
                   shape(tokens, state), shape(1, heads), shape(1, heads), shape(1, heads)],
        scratch_shapes=list(scratch.values()),
        compiler_params=pltpu.CompilerParams(
            collective_id=0, has_side_effects=True, vmem_limit_bytes=60 << 20),
        name="layer",
    )(tokens_x, grad_y, raw_dt, step_bias[None], decay_rate[None], skip_gain[None], in_b, in_c)
    return gx, graw, gb, gc, grate[0], gskip[0], gbias[0]


def solution(mesh):
    return jax.shard_map(
        functools.partial(on_device, mesh.shape["ctx"], mesh.shape["head"]),
        mesh=mesh,
        in_specs=(
            P("ctx", "head"),
            P("head", "ctx"),
            P("ctx", None),
            P("ctx", None),
            P("head"),
            P("head"),
            P("head"),
            P("ctx", "head"),
        ),
        out_specs=(
            P("ctx", "head"),
            P("head", "ctx"),
            P("ctx", None),
            P("ctx", None),
            P("head"),
            P("head"),
            P("head"),
        ),
        check_vma=False,
    )
```

profile of v0, /device:TPU:0, one launch (start us, length us, event | category | flops | bytes accessed | tf_op | source)
XLA Modules:
  0.0 74.9 jit_solution(11085919269216023342)
XLA Ops:
  0.6 67.4 %layer.1 = (bf16[512,2048]{1,0:T(8,128)(2,1)}, f32[32,512]{1,0:T(8,128)}, f32[512,128]{1,0:T(8,128)}, f32[512,128]{1,0:T(8,128)}, f32[1,32]{1,0:T(1,128)}, /*index=5*/f32[1,32]{1,0:T(1,128)}, f32[1,32]{1,0:T(1,128)}) custom-call(bf16[512,2048]{1,0:T(8,128)(2,1)} %refs_0_.1, bf16[512,2048]{1,0:T(8,128)(2,1)} %refs_1_.1, f32[32,512]{1,0:T(8,128)} %refs_2_.1, ...), custom_call_target="tpu_custom_call" | custom-call | tf_op jit(solution)/shard_map/layer/pallas_call | solution.py:618
  68.1 0.0 copy-start.2
  68.1 0.0 copy-start.1
  68.1 0.0 copy-start
  68.1 0.0 copy-start.5
  68.1 0.0 copy-start.4
  68.1 0.0 copy-start.3
  68.1 3.2 %copy.22 = bf16[512,2048]{1,0:T(8,128)(2,1)} copy(bf16[512,2048]{1,0:T(8,128)(2,1)} %get-tuple-element.28) | data formatting | bytes 4194304
  71.4 0.0 copy-done.2
  71.4 0.6 copy.23
  72.0 0.0 copy-done.1
  72.0 0.7 copy.24
  72.7 0.0 copy-done
  72.7 0.7 copy.25
  73.4 0.0 copy-done.5
  73.4 0.5 copy.26
  73.9 0.0 copy-done.4
  73.9 0.5 copy.27
  74.4 0.0 copy-done.3
  74.4 0.5 copy.28
Async XLA Ops:
  68.1 3.3 %copy-start.2 = (f32[32,512]{1,0:T(8,128)S(1)}, f32[32,512]{1,0:T(8,128)}, u32[]{:S(2)}) copy-start(f32[32,512]{1,0:T(8,128)} %get-tuple-element.29) | copy-start | bytes 196612
  68.1 3.9 %copy-start.1 = (f32[512,128]{1,0:T(8,128)S(1)}, f32[512,128]{1,0:T(8,128)}, u32[]{:S(2)}) copy-start(f32[512,128]{1,0:T(8,128)} %get-tuple-element.30) | copy-start | bytes 786436
  68.1 4.6 %copy-start = (f32[512,128]{1,0:T(8,128)S(1)}, f32[512,128]{1,0:T(8,128)}, u32[]{:S(2)}) copy-start(f32[512,128]{1,0:T(8,128)} %get-tuple-element.31) | copy-start | bytes 786436
  68.1 5.3 %copy-start.5 = (f32[1,32]{1,0:T(1,128)S(1)}, f32[1,32]{1,0:T(1,128)}, u32[]{:S(2)}) copy-start(f32[1,32]{1,0:T(1,128)} %get-tuple-element.18) | copy-start | bytes 388
  68.1 5.8 %copy-start.4 = (f32[1,32]{1,0:T(1,128)S(1)}, f32[1,32]{1,0:T(1,128)}, u32[]{:S(2)}) copy-start(f32[1,32]{1,0:T(1,128)} %get-tuple-element.19) | copy-start | bytes 388
  68.1 6.3 %copy-start.3 = (f32[1,32]{1,0:T(1,128)S(1)}, f32[1,32]{1,0:T(1,128)}, u32[]{:S(2)}) copy-start(f32[1,32]{1,0:T(1,128)} %get-tuple-element.20) | copy-start | bytes 388
where the time goes:
time: 75.1 us; the launch traced here: 74.9 us
  Pallas kernels  67.4 us (90%)
  local copies, waits for them, and re-layouts  6.81 us (9%)
    pallas_call x1, Pallas kernels, on_device(): pl.pallas_call(functools.partial(kernel, names, peers, line), in_specs=[h...  67.4 us
    unnamed x19, local copies, waits for them, and re-layouts  6.81 us

commit v1 on v0

v1 whole, which is shorter than its diff:
```python
import functools
import types

import jax
import jax.numpy as jnp
from jax import lax
from jax.experimental import pallas as pl
from jax.experimental.pallas import tpu as pltpu
from jax.sharding import PartitionSpec as P

CHUNK = 128
GROUP = 8
F32 = jnp.float32
BF16 = jnp.bfloat16
HIGH = lax.Precision.HIGHEST
NT = (((1,), (1,)), ((), ()))
MESH = pl.DeviceIdType.MESH
VMEM_LIMIT = 50 << 20


def mm(a, b):
    return jnp.dot(a, b, preferred_element_type=F32)


def mm_nt(a, b):
    return lax.dot_general(a, b, NT, preferred_element_type=F32)


def split(a):
    high = a.astype(BF16)
    return high, (a - high.astype(F32)).astype(BF16)


def twice(a, axis):
    return jnp.concatenate([a, a], axis=axis)


def softplus(v):
    return jnp.maximum(v, 0.0) + jnp.log1p(jnp.exp(-jnp.abs(v)))


def lanes(column, width=CHUNK):
    return jnp.broadcast_to(column, (column.shape[0], width))


def per_head(rows, matrix):
    heads = rows.shape[0]
    shaped = matrix.reshape(heads, matrix.shape[0] // heads, matrix.shape[1])
    return (shaped * rows[:, None, :]).reshape(matrix.shape)


def head_sums(matrix, heads):
    return jnp.sum(matrix.reshape(heads, matrix.shape[0] // heads, matrix.shape[1]), axis=1)


def pair_blocks(first, second):
    zero = jnp.zeros_like(first)
    return jnp.concatenate(
        [jnp.concatenate([first, zero], axis=1), jnp.concatenate([zero, second], axis=1)], axis=0
    )


def triangle(lower):
    row = lax.broadcasted_iota(jnp.int32, (CHUNK, CHUNK), 0)
    col = lax.broadcasted_iota(jnp.int32, (CHUNK, CHUNK), 1)
    return (row >= col) if lower else (row <= col)


def eye(n):
    row = lax.broadcasted_iota(jnp.int32, (n, n), 0)
    col = lax.broadcasted_iota(jnp.int32, (n, n), 1)
    return row == col


def column_of(row):
    n = row.shape[1]
    return jnp.sum(jnp.where(eye(n), jnp.broadcast_to(row, (n, n)), 0.0), axis=1, keepdims=True)


def row_of(column):
    n = column.shape[0]
    return jnp.sum(jnp.where(eye(n), jnp.broadcast_to(column, (n, n)), 0.0), axis=0, keepdims=True)


def span_of(c):
    return slice(c * CHUNK, (c + 1) * CHUNK)


def inputs_and_outputs():
    return ("x_hbm", "g_hbm", "raw", "bias", "rate", "skip", "b", "c",
            "gx", "graw", "ztot", "grate", "gskip", "gbias")


def scratch_of(heads, tokens, size, state, peers):
    groups, chunks, chips = heads // GROUP, tokens // CHUNK, peers // 2
    wide, half = GROUP * size, size // 2
    vmem = pltpu.VMEM
    dma = pltpu.SemaphoreType.DMA
    halves = (2, groups, GROUP, half, state)
    segments = (2, chunks, CHUNK, state)
    return dict(
        src=vmem((2, groups, tokens, wide), BF16),
        xt=vmem((groups, wide, tokens), BF16),
        gt=vmem((groups, wide, tokens), BF16),
        dt=vmem((heads, tokens), F32),
        cum=vmem((heads, tokens), F32),
        scale=vmem((2, heads, tokens), F32),
        step=vmem((chunks, heads, CHUNK), F32),
        edge=vmem((2, chunks, heads, CHUNK), F32),
        whole=vmem((heads, CHUNK), F32),
        skips=vmem((heads, CHUNK), F32),
        local=vmem((2, groups, chunks, wide, state), F32),
        total=vmem((2, groups, GROUP, size, state), F32),
        ends=vmem((peers, heads, CHUNK), F32),
        coef=vmem((2, chips, heads, CHUNK), F32),
        pair_in=vmem(halves, F32),
        agg=vmem(halves, F32),
        chip_in=vmem((chips,) + halves[1:], F32),
        pre=vmem(halves, F32),
        give=vmem(halves, F32),
        state_in=vmem((2, groups, GROUP, size, state), F32),
        dxt=vmem((groups, chunks, wide, CHUNK), F32),
        row=vmem((groups, chunks, GROUP, CHUNK), F32),
        col=vmem((groups, chunks, GROUP, CHUNK), F32),
        cross=vmem((groups, GROUP, CHUNK), F32),
        dg=vmem((chunks, CHUNK, CHUNK), F32),
        parts=vmem((2, groups, chunks, 2, wide, state), BF16),
        zown=vmem(segments, F32),
        zsum=vmem(segments, F32),
        zin=vmem((2,) + segments, F32),
        params_in=vmem((peers, heads, CHUNK), F32),
        load_sem=dma((2, groups)),
        end_send=dma((peers,)),
        end_recv=dma((peers,)),
        pair_send=dma((2, groups)),
        pair_recv=dma((2, groups)),
        chip_send=dma((chips, groups)),
        chip_recv=dma((chips, groups)),
        back_send=dma((2, groups)),
        back_recv=dma((2, groups)),
        in_send=dma((2, chunks)),
        out_send=dma((2, chunks)),
        z_recv=dma((2, 2, chunks)),
        param_send=dma((peers,)),
        param_recv=dma((peers,)),
    )


def kernel(names, peers, line, *refs):
    k = types.SimpleNamespace(**dict(zip(names, refs)))
    heads, tokens = k.raw.shape
    state = k.b.shape[1]
    groups, chunks, chips = heads // GROUP, tokens // CHUNK, peers // 2
    wide = k.src.shape[3]
    size = wide // GROUP
    half = size // 2
    me, zpos = lax.axis_index("ctx"), lax.axis_index("head")
    odd, chip = me % 2, me // 2
    mate = me + 1 - 2 * odd
    early = jnp.where(chip < chips // 2, 0, 1)
    late = 1 - early

    left = zpos < line // 2
    inner = jnp.where(left, zpos + 1, zpos - 1)
    outer = jnp.where(left, zpos - 1, zpos + 1)
    has_outer = jnp.logical_and(zpos > 0, zpos < line - 1)
    is_mid = jnp.logical_or(zpos == line // 2 - 1, zpos == line // 2)
    in_slot = jnp.where(is_mid, 1, 0)

    barrier = pltpu.get_barrier_semaphore()

    def remote(src, dst, send, recv, **place):
        return pltpu.make_async_remote_copy(
            src_ref=src, dst_ref=dst, send_sem=send, recv_sem=recv,
            device_id=place, device_id_type=MESH)

    def greet():
        for d in range(1, peers):
            pl.semaphore_signal(barrier, inc=1, device_id={"ctx": (me + d) % peers}, device_id_type=MESH)
        pl.semaphore_signal(barrier, inc=1, device_id={"head": inner}, device_id_type=MESH)

        @pl.when(has_outer)
        def _():
            pl.semaphore_signal(barrier, inc=1, device_id={"head": outer}, device_id_type=MESH)

    def met():
        pl.semaphore_wait(barrier, peers + jnp.where(has_outer, 1, 0))

    def load(e, group):
        at = pl.ds(pl.multiple_of(group * wide, wide), wide)
        return pltpu.make_async_copy((k.g_hbm, k.x_hbm)[e].at[:, at], k.src.at[e, group], k.load_sem.at[e, group])

    def start_loads():
        for group in range(groups):
            load(1, group).start()
            load(0, group).start()

    def prepare():
        dt = softplus(k.raw[...] + column_of(k.bias[...]))
        k.dt[...] = dt
        log_decay = -column_of(k.rate[...]) * dt
        ones = triangle(False).astype(F32)
        cums = [jnp.dot(log_decay[:, span_of(c)], ones, precision=HIGH) for c in range(chunks)]
        ends = [lanes(cum[:, CHUNK - 1:]) for cum in cums]
        before, after = jnp.zeros_like(ends[0]), jnp.zeros_like(ends[0])
        for c in range(chunks):
            k.edge[0, c] = jnp.exp(before)
            before = before + ends[c]
            k.edge[1, chunks - 1 - c] = jnp.exp(after)
            after = after + ends[chunks - 1 - c]
        k.whole[...] = jnp.exp(before)
        k.ends[me] = before
        for c in range(chunks):
            k.cum[:, span_of(c)] = cums[c]
            k.scale[0, :, span_of(c)] = jnp.exp(cums[c])
            k.scale[1, :, span_of(c)] = jnp.exp(ends[c] - cums[c]) * dt[:, span_of(c)]
            k.step[c] = jnp.exp(ends[c])
        k.dg[...] = jnp.zeros_like(k.dg)
        k.skips[...] = lanes(column_of(k.skip[...]))

    def end_copy(d, place):
        return remote(k.ends.at[place], k.ends.at[place], k.end_send.at[d], k.end_recv.at[d],
                      ctx=(me + d) % peers)

    def send_ends():
        for d in range(1, peers):
            end_copy(d, me).start()

    mine = pl.ds(pl.multiple_of(odd * half, half), half)
    theirs = pl.ds(pl.multiple_of((1 - odd) * half, half), half)

    def pair_copy(e, group):
        return remote(k.total.at[e, group, :, theirs, :], k.pair_in.at[e, group],
                      k.pair_send.at[e, group], k.pair_recv.at[e, group], ctx=mate)

    def chip_copy(step, group):
        what = jnp.where(chip + step < chips, 0, 1)
        return remote(k.agg.at[what, group], k.chip_in.at[step, group],
                      k.chip_send.at[step, group], k.chip_recv.at[step, group], ctx=(me + 2 * step) % peers)

    def back_copy(e, group, rows):
        return remote(k.give.at[e, group], k.state_in.at[e, group, :, rows, :],
                      k.back_send.at[e, group], k.back_recv.at[e, group], ctx=mate)

    def rows_of(group):
        return pl.ds(pl.multiple_of(group * GROUP, GROUP), GROUP)

    def carry_local(e, group, order, source, operand):
        at_rows = rows_of(group)
        value = None
        for c in order:
            at = span_of(c)
            k.local[e, group, c] = jnp.zeros((wide, state), F32) if value is None else value
            high, low = split(per_head(k.scale[1 - e, at_rows, at], source[group, :, at].astype(F32)))
            added = mm(jnp.concatenate([high, low], axis=1), twice(operand[at, :], 0))
            value = added if value is None else per_head(k.step[c, at_rows], value) + added
        k.total[e, group] = value.reshape(GROUP, size, state)

    def states(group):
        load(1, group).wait()
        k.xt[group] = k.src[1, group].T
        carry_local(0, group, range(chunks), k.xt, k.b)

    def backs(group):
        load(0, group).wait()
        k.gt[group] = k.src[0, group].T
        carry_local(1, group, reversed(range(chunks)), k.gt, k.c)

    def make_coefs():
        for d in range(1, peers):
            @pl.when(d != mate_step)
            def _():
                end_copy(d, (me - d + peers) % peers).wait_recv()
        s_log = jnp.zeros((heads, CHUNK), F32)
        r_log = jnp.zeros((heads, CHUNK), F32)
        for step in range(1, chips):
            k.coef[0, step] = jnp.exp(s_log)
            k.coef[1, step] = jnp.exp(r_log)
            low = (chip - step + chips) % chips
            high = (chip + step) % chips
            s_log = s_log + (k.ends[2 * low] + k.ends[2 * low + 1])
            r_log = r_log + (k.ends[2 * high] + k.ends[2 * high + 1])

    def scaled(coef, block):
        return coef[:, None, :] * block

    def downstream(e):
        return jnp.where(e == 0, odd, 1 - odd) == 1

    def own_and_mate(group):
        at_rows = rows_of(group)
        own = jnp.exp(k.ends[me, at_rows])
        return own, jnp.exp(k.ends[mate, at_rows]), jnp.ones_like(own), jnp.zeros_like(own)

    def combine(group):
        @pl.when(group == 0)
        def _():
            end_copy(mate_step, mate).wait_recv()

        own_e, mate_e, one, _ = own_and_mate(group)
        for e in range(2):
            down = downstream(e)
            pair_copy(e, group).wait_recv()
            k.agg[e, group] = (scaled(jnp.where(down, one, mate_e), k.total[e, group, :, mine, :])
                               + scaled(jnp.where(down, own_e, one), k.pair_in[e, group]))

    def finalize(e, group):
        at_rows = rows_of(group)
        k.pre[e, group] = jnp.zeros((GROUP, half, state), F32)
        for step in range(1, chips):
            slot = jnp.where(e == 0, step, chips - step)

            @pl.when(jnp.where(e == 0, chip, chips - 1 - chip) >= step)
            def _():
                chip_copy(slot, group).wait_recv()
                k.pre[e, group] += scaled(k.coef[e, step, at_rows], k.chip_in[slot, group])

        own_e, mate_e, one, zero = own_and_mate(group)
        down = downstream(e)
        pre = k.pre[e, group]
        k.give[e, group] = (scaled(jnp.where(down, one, own_e), pre)
                            + scaled(jnp.where(down, zero, one), k.total[e, group, :, mine, :]))
        k.state_in[e, group, :, mine, :] = (scaled(jnp.where(down, mate_e, one), pre)
                                            + scaled(jnp.where(down, one, zero), k.pair_in[e, group]))
        back_copy(e, group, mine).start()

    causal = triangle(False)

    def within(group):
        def one_chunk(c, carry):
            at = pl.ds(pl.multiple_of(c * CHUNK, CHUNK), CHUNK)
            scores = mm_nt(k.b[at, :], k.c[at, :])
            cum = k.cum[rows_of(group), at]
            shifted = (cum - jnp.log(k.dt[rows_of(group), at])).T
            total = jnp.zeros((CHUNK, CHUNK), F32)
            rows, cols = [], []
            for pair in range(GROUP // 2):
                x_pair = k.src[1, group, at, pair * 2 * size:(pair + 1) * 2 * size]
                places = [slice((2 * pair + j) * size, (2 * pair + j + 1) * size) for j in range(2)]
                products = mm(x_pair, pair_blocks(k.gt[group, places[0], at], k.gt[group, places[1], at]))
                for j in range(2):
                    h = 2 * pair + j
                    gap = cum[h:h + 1, :] - shifted[:, h:h + 1]
                    decay = jnp.exp(jnp.where(causal, gap, -1e30))
                    both = products[:, j * CHUNK:(j + 1) * CHUNK] * decay
                    total = total + both
                    rows.append(jnp.sum(both * scores, axis=0, keepdims=True))
                    high, low = split(decay * scores)
                    dx_h = mm_nt(twice(k.gt[group, places[j], at], 1), jnp.concatenate([high, low], axis=1))
                    k.dxt[group, c, places[j], :] = dx_h
                    x_h = k.xt[group, places[j], at]
                    cols.append(jnp.sum(dx_h * x_h.astype(F32), axis=0, keepdims=True))
            k.row[group, c] = jnp.concatenate(rows, axis=0)
            k.col[group, c] = jnp.concatenate(cols, axis=0)
            k.dg[c] += total
            return carry

        lax.fori_loop(0, chunks, one_chunk, 0)

    def score_parts():
        for c in range(chunks):
            at = span_of(c)
            for e, dg, operand in ((0, k.dg[c].T, k.b), (1, k.dg[c], k.c)):
                high, low = split(dg)
                k.zown[e, c] = mm(jnp.concatenate([high, low], axis=1), twice(operand[at, :], 0))

    def projections(e, c):
        at = span_of(c)
        total = k.zown[e, c]
        for group in range(groups):
            if c == 0:
                back_copy(e, group, theirs).wait_recv()
            at_rows = rows_of(group)
            incoming = k.state_in[e, group].reshape(wide, state)
            high, low = split(per_head(k.edge[e, c, at_rows], incoming) + k.local[e, group, c])
            k.parts[e, group, c, 0] = high
            k.parts[e, group, c, 1] = low
            column = k.scale[e, at_rows, at].T
            for pair in range(GROUP // 2):
                wide_at = slice(pair * 2 * size, (pair + 1) * 2 * size)
                one = slice(2 * pair * size, (2 * pair + 1) * size)
                two = slice((2 * pair + 1) * size, (2 * pair + 2) * size)
                both = mm(twice(k.src[e, group, at, wide_at], 1),
                          jnp.concatenate([pair_blocks(high[one], high[two]),
                                           pair_blocks(low[one], low[two])], axis=0))
                for j in range(2):
                    h = 2 * pair + j
                    total = total + both[:, j * state:(j + 1) * state] * column[:, h:h + 1]
        k.zown[e, c] = total

    def inward(e, c, source):
        return remote(source.at[e, c], k.zin.at[in_slot, e, c],
                      k.in_send.at[e, c], k.z_recv.at[in_slot, e, c], head=inner)

    def outward(e, c, slot=1):
        return remote(k.ztot.at[e, c], k.zin.at[slot, e, c],
                      k.out_send.at[e, c], k.z_recv.at[slot, e, c], head=outer)

    def publish(e, c):
        @pl.when(jnp.logical_not(has_outer))
        def _():
            inward(e, c, k.zown).start()

    def relay(e, c):
        @pl.when(has_outer)
        def _():
            outward(e, c, 0).wait_recv()
            k.zsum[e, c] = k.zown[e, c] + k.zin[0, e, c]
            inward(e, c, k.zsum).start()

    def settle(e, c):
        outward(e, c).wait_recv()

        @pl.when(jnp.logical_and(is_mid, has_outer))
        def _():
            k.ztot[e, c] = k.zsum[e, c] + k.zin[1, e, c]

        @pl.when(jnp.logical_and(is_mid, jnp.logical_not(has_outer)))
        def _():
            k.ztot[e, c] = k.zown[e, c] + k.zin[1, e, c]

        @pl.when(jnp.logical_not(is_mid))
        def _():
            k.ztot[e, c] = k.zin[1, e, c]

        @pl.when(has_outer)
        def _():
            outward(e, c).start()

    def settle_mid(e, c):
        @pl.when(is_mid)
        def _():
            settle(e, c)

    def settle_rest(e, c):
        @pl.when(jnp.logical_not(is_mid))
        def _():
            settle(e, c)

    def inputs_step(c, group):
        at, at_rows = span_of(c), rows_of(group)
        bb, cc = twice(k.b[at, :], 1), twice(k.c[at, :], 1)
        reach, weight = k.scale[0, at_rows, at], k.scale[1, at_rows, at]
        xt, gt = k.xt[group, :, at].astype(F32), k.gt[group, :, at].astype(F32)
        parts = [jnp.concatenate([k.parts[e, group, c, 0], k.parts[e, group, c, 1]], axis=1) for e in range(2)]
        y = mm_nt(parts[0], cc)
        k.row[group, c] += head_sums(y * gt, GROUP) * reach
        dx = per_head(weight, mm_nt(parts[1], bb))
        k.col[group, c] += head_sums(dx * xt, GROUP)
        product = head_sums(xt * gt, GROUP)
        k.cross[group] = product if c == 0 else k.cross[group] + product
        dx = dx + k.dxt[group, c] + per_head(k.skips[at_rows], gt)
        k.gx[group, c] = dx.astype(BF16).T

    def step_sizes():
        rate, bias = column_of(k.rate[...]), column_of(k.bias[...])
        beyond = []
        for group in range(groups):
            last = k.total[0, group] + scaled(k.whole[rows_of(group)], k.state_in[0, group])
            sums = jnp.sum(last * k.state_in[1, group], axis=1)
            beyond.append(jnp.sum(sums, axis=1, keepdims=True))
        beyond = lanes(jnp.concatenate(beyond, axis=0))
        suffix = triangle(True).astype(F32)
        g_rate = jnp.zeros((heads, 1), F32)
        g_bias = jnp.zeros((heads, 1), F32)
        for c in reversed(range(chunks)):
            at = span_of(c)
            row = jnp.concatenate([k.row[group, c] for group in range(groups)], axis=0)
            col = jnp.concatenate([k.col[group, c] for group in range(groups)], axis=0)
            change = row - col
            d_log = jnp.dot(change, suffix, precision=HIGH) + beyond
            beyond = beyond + lanes(jnp.sum(change, axis=1, keepdims=True))
            dt = k.dt[:, at]
            g_dt = col / dt - rate * d_log
            g_raw = g_dt / (1.0 + jnp.exp(-(k.raw[:, at] + bias)))
            k.graw[:, at] = g_raw
            g_rate = g_rate - jnp.sum(dt * d_log, axis=1, keepdims=True)
            g_bias = g_bias + jnp.sum(g_raw, axis=1, keepdims=True)
        cross = jnp.concatenate([k.cross[group] for group in range(groups)], axis=0)
        g_skip = jnp.sum(cross, axis=1, keepdims=True)
        lane = lax.broadcasted_iota(jnp.int32, (heads, CHUNK), 1)
        k.params_in[me] = jnp.where(lane == 0, g_rate, jnp.where(lane == 1, g_skip, g_bias))

    def params_copy(d, place):
        return remote(k.params_in.at[place], k.params_in.at[place], k.param_send.at[d], k.param_recv.at[d],
                      ctx=(me + d) % peers)

    def gather_params():
        for d in range(1, peers):
            params_copy(d, (me - d + peers) % peers).wait_recv()
        total = k.params_in[0]
        for d in range(1, peers):
            total = total + k.params_in[d]
        k.grate[...] = row_of(total[:, 0:1])
        k.gskip[...] = row_of(total[:, 1:2])
        k.gbias[...] = row_of(total[:, 2:3])

    mate_step = jnp.where(odd == 1, 1, peers - 1)

    def nth_step(n):
        return jnp.where(chip < chips // 2, n, chips - n)

    def exchange(group):
        combine(group)
        for n in range(1, min(3, chips)):
            chip_copy(nth_step(n), group).start()

    def first_step(group, carry):
        states(group)
        pair_copy(0, group).start()
        backs(group)
        pair_copy(1, group).start()

        @pl.when(group > 0)
        def _():
            exchange(group - 1)

        return carry

    greet()
    start_loads()
    prepare()
    met()
    send_ends()
    lax.fori_loop(0, groups, first_step, 0)

    done = 0
    for group in range(groups):
        within(group)
        if group == 0:
            exchange(groups - 1)
            for n in range(3, chips):
                lax.fori_loop(0, groups, lambda group, carry: (chip_copy(nth_step(n), group).start(), carry)[1], 0)
            make_coefs()
        if group >= 1 or groups == 1:
            while done < min(group + 1, groups) and (group == groups - 1 or done < group):
                finalize(early, done)
                done += 1
    score_parts()

    pieces = [(e, c) for e in (early, late) for c in range(chunks)]
    relayed, settled = 0, 0

    def tend(relays, settles):
        nonlocal relayed, settled
        while relayed < min(relays, len(pieces)):
            relay(*pieces[relayed])
            relayed += 1
        while settled < min(settles, relayed):
            settle_mid(*pieces[settled])
            settled += 1

    for c in range(chunks):
        projections(early, c)
        publish(early, c)
    for group in range(groups):
        finalize(late, group)
        tend(min(group, 3), 0)
    for c in range(chunks):
        projections(late, c)
        publish(late, c)
        tend(chunks, (1, 2, 3, 4)[min(c, 3)])
    turns = [(c, group) for c in range(chunks) for group in range(groups)]
    for j, turn in enumerate(turns):
        inputs_step(*turn)
        part = 16 * (j + 1) // len(turns)
        tend(chunks + sum(part >= at for at in (2, 6, 10, 13)), chunks + sum(part >= at for at in (10, 14)))
    tend(len(pieces), 0)
    step_sizes()
    for d in range(1, peers):
        params_copy(d, me).start()
    tend(len(pieces), len(pieces))
    for piece in pieces:
        settle_rest(*piece)
    gather_params()

    def drain():
        for group in range(groups):
            for e in range(2):
                pair_copy(e, group).wait_send()
                back_copy(e, group, mine).wait_send()
            for step in range(1, chips):
                chip_copy(step, group).wait_send()
        for c in range(chunks):
            for e in range(2):
                inward(e, c, k.zsum).wait_send()

                @pl.when(has_outer)
                def _():
                    outward(e, c).wait_send()
        for d in range(1, peers):
            end_copy(d, me).wait_send()
            params_copy(d, me).wait_send()

    drain()


def finish_kernel(groups, chunks, gx, graw, ztot, grate, gskip, gbias,
                  gx_out, graw_out, gb_out, gc_out, grate_out, gskip_out, gbias_out, sems):
    wide = gx.shape[3]
    copies = [(gx.at[group, c], gx_out.at[span_of(c), group * wide:(group + 1) * wide])
              for group in range(groups) for c in range(chunks)]
    copies += [(ztot.at[1 - i, c], ref.at[span_of(c), :]) for i, ref in enumerate((gb_out, gc_out))
               for c in range(chunks)]
    copies += [(graw, graw_out), (grate, grate_out), (gskip, gskip_out), (gbias, gbias_out)]
    copies = [pltpu.make_async_copy(src, dst, sems.at[i]) for i, (src, dst) in enumerate(copies)]
    for copy in copies:
        copy.start()
    for copy in copies:
        copy.wait()


def on_device(peers, line, tokens_x, raw_dt, in_b, in_c, decay_rate, skip_gain, step_bias, grad_y):
    heads, tokens = raw_dt.shape
    width = tokens_x.shape[1]
    size = width // heads
    state = in_b.shape[1]
    groups, chunks = heads // GROUP, tokens // CHUNK
    scratch = scratch_of(heads, tokens, size, state, peers)
    names = inputs_and_outputs() + tuple(scratch)

    def shape(*dims, dtype=F32):
        return jax.ShapeDtypeStruct(dims, dtype)

    hbm, vmem = pl.BlockSpec(memory_space=pl.ANY), pl.BlockSpec(memory_space=pltpu.VMEM)
    row = shape(1, heads)
    results = pl.pallas_call(
        functools.partial(kernel, names, peers, line),
        in_specs=[hbm, hbm] + [vmem] * 6,
        out_specs=[vmem] * 6,
        out_shape=[shape(groups, chunks, CHUNK, GROUP * size, dtype=BF16), shape(heads, tokens),
                   shape(2, chunks, CHUNK, state), row, row, row],
        scratch_shapes=list(scratch.values()),
        compiler_params=pltpu.CompilerParams(
            collective_id=0, has_side_effects=True, vmem_limit_bytes=VMEM_LIMIT),
        name="layer",
    )(tokens_x, grad_y, raw_dt, step_bias[None], decay_rate[None], skip_gain[None], in_b, in_c)
    gx, graw, gb, gc, grate, gskip, gbias = pl.pallas_call(
        functools.partial(finish_kernel, groups, chunks),
        in_specs=[vmem] * 6,
        out_specs=[hbm] * 7,
        out_shape=[shape(tokens, width, dtype=BF16), shape(heads, tokens), shape(tokens, state),
                   shape(tokens, state), row, row, row],
        scratch_shapes=[pltpu.SemaphoreType.DMA((groups * chunks + 2 * chunks + 4,))],
        compiler_params=pltpu.CompilerParams(vmem_limit_bytes=4 << 20),
        name="finish",
    )(*results)
    return gx, graw, gb, gc, grate[0], gskip[0], gbias[0]


def solution(mesh):
    return jax.shard_map(
        functools.partial(on_device, mesh.shape["ctx"], mesh.shape["head"]),
        mesh=mesh,
        in_specs=(
            P("ctx", "head"),
            P("head", "ctx"),
            P("ctx", None),
            P("ctx", None),
            P("head"),
            P("head"),
            P("head"),
            P("ctx", "head"),
        ),
        out_specs=(
            P("ctx", "head"),
            P("head", "ctx"),
            P("ctx", None),
            P("ctx", None),
            P("head"),
            P("head"),
            P("head"),
        ),
        check_vma=False,
    )
```

time: 75.1 us -> 57.9 us (0.77)
  Pallas kernels: 67.4 us -> 52.3 us
  local copies, waits for them, and re-layouts: 6.81 us -> 4.6 us
    pallas_call x1, Pallas kernels: 67.4 us -> 50.5 us  [on_device(): pl.pallas_call(functools.partial(kernel, names, peers, line), in_specs=[h...]
    unnamed x19 -> x12, local copies, waits for them, and re-layouts: 6.81 us -> 4.6 us
    pallas_call x0 -> x1, Pallas kernels: none -> 1.74 us  [on_device(): pl.pallas_call(functools.partial(finish_kernel, groups, chunks), in_specs...]
where the time goes in v1:
time: 57.9 us; the launch traced here: 57.7 us
  Pallas kernels  52.3 us (90%)
  local copies, waits for them, and re-layouts  4.6 us (8%)
  between operations  0.82 us (1%)
    pallas_call x1, Pallas kernels, on_device(): pl.pallas_call(functools.partial(kernel, names, peers, line), in_specs=[h...  50.5 us
    unnamed x12, local copies, waits for them, and re-layouts  4.6 us
    pallas_call x1, Pallas kernels, on_device(): pl.pallas_call(functools.partial(finish_kernel, groups, chunks), in_specs...  1.74 us

profile of v1, /device:TPU:0, one launch (start us, length us, event | category | flops | bytes accessed | tf_op | source)
XLA Modules:
  0.0 57.7 jit_solution(1633336483157484853)
XLA Ops:
  0.6 0.0 copy-start
  0.6 0.9 %copy-done = bf16[512,128]{1,0:T(8,128)(2,1)S(1)} copy-done((bf16[512,128]{1,0:T(8,128)(2,1)S(1)}, bf16[512,128]{1,0:T(8,128)(2,1)}, u32[]{:S(2)}) %copy-start) | copy-done | bytes 131096
  1.5 0.0 copy-start.1
  1.5 0.9 %copy-done.1 = bf16[512,128]{1,0:T(8,128)(2,1)S(1)} copy-done((bf16[512,128]{1,0:T(8,128)(2,1)S(1)}, bf16[512,128]{1,0:T(8,128)(2,1)}, u32[]{:S(2)}) %copy-start.1) | copy-done | bytes 131096
  2.4 0.0 copy-start.2
  2.4 0.8 %copy-done.2 = f32[32,512]{1,0:T(8,128)S(1)} copy-done((f32[32,512]{1,0:T(8,128)S(1)}, f32[32,512]{1,0:T(8,128)}, u32[]{:S(2)}) %copy-start.2) | copy-done | bytes 65560
  3.3 0.0 copy-start.3
  3.3 0.7 %copy-done.3 = f32[32]{0:T(128)S(1)} copy-done((f32[32]{0:T(128)S(1)}, f32[32]{0:T(128)}, u32[]{:S(2)}) %copy-start.3) | copy-done | bytes 152
  3.9 0.0 copy-start.4
  3.9 0.7 %copy-done.4 = f32[32]{0:T(128)S(1)} copy-done((f32[32]{0:T(128)S(1)}, f32[32]{0:T(128)}, u32[]{:S(2)}) %copy-start.4) | copy-done | bytes 152
  4.6 0.0 copy-start.5
  4.6 0.7 %copy-done.5 = f32[32]{0:T(128)S(1)} copy-done((f32[32]{0:T(128)S(1)}, f32[32]{0:T(128)}, u32[]{:S(2)}) %copy-start.5) | copy-done | bytes 152
  5.3 50.5 %layer.1 = (bf16[4,4,128,512]{3,2,1,0:T(8,128)(2,1)S(1)}, f32[32,512]{1,0:T(8,128)S(1)}, f32[2,4,128,128]{3,2,1,0:T(8,128)S(1)}, f32[1,32]{1,0:T(1,128)S(1)}, f32[1,32]{1,0:T(1,128)S(1)}, /*index=5*/f32[1,32]{1,0:T(1,128)S(1)}) custom-call(bf16[512,2048]{1,0:T(8,128)(2,1)} %refs_0_.1, bf16[512,2048]{1,0:T(8,128)(2,1)} %refs_1_.1, f32[32,512]{1,0:T(8,128)S(1)} %copy-done.2, ...), custom_call_target="tpu_custom_call" | custom-call | tf_op jit(solution)/shard_map/layer/pallas_call | solution.py:627
  55.8 1.7 %finish.1 = (bf16[512,2048]{1,0:T(8,128)(2,1)}, f32[32,512]{1,0:T(8,128)}, f32[512,128]{1,0:T(8,128)}, f32[512,128]{1,0:T(8,128)}, f32[1,32]{1,0:T(1,128)}, /*index=5*/f32[1,32]{1,0:T(1,128)}, f32[1,32]{1,0:T(1,128)}) custom-call(bf16[4,4,128,512]{3,2,1,0:T(8,128)(2,1)S(1)} %get-tuple-element.20.gx, f32[32,512]{1,0:T(8,128)S(1)} %get-tuple-element.21.graw, ...), custom_call_target="tpu_custom_call" | custom-call | tf_op jit(solution)/shard_map/finish/pallas_call | solution.py:638
Async XLA Ops:
  0.6 0.9 %copy-start = (bf16[512,128]{1,0:T(8,128)(2,1)S(1)}, bf16[512,128]{1,0:T(8,128)(2,1)}, u32[]{:S(2)}) copy-start(bf16[512,128]{1,0:T(8,128)(2,1)} %refs_6_.1) | copy-start | bytes 393220
  1.5 0.9 %copy-start.1 = (bf16[512,128]{1,0:T(8,128)(2,1)S(1)}, bf16[512,128]{1,0:T(8,128)(2,1)}, u32[]{:S(2)}) copy-start(bf16[512,128]{1,0:T(8,128)(2,1)} %refs_7_.1) | copy-start | bytes 393220
  2.4 0.8 %copy-start.2 = (f32[32,512]{1,0:T(8,128)S(1)}, f32[32,512]{1,0:T(8,128)}, u32[]{:S(2)}) copy-start(f32[32,512]{1,0:T(8,128)} %refs_2_.1) | copy-start | bytes 196612
  3.3 0.7 %copy-start.3 = (f32[32]{0:T(128)S(1)}, f32[32]{0:T(128)}, u32[]{:S(2)}) copy-start(f32[32]{0:T(128)} %param.14) | copy-start | bytes 388
  3.9 0.7 %copy-start.4 = (f32[32]{0:T(128)S(1)}, f32[32]{0:T(128)}, u32[]{:S(2)}) copy-start(f32[32]{0:T(128)} %param.12) | copy-start | bytes 388
  4.6 0.7 %copy-start.5 = (f32[32]{0:T(128)S(1)}, f32[32]{0:T(128)}, u32[]{:S(2)}) copy-start(f32[32]{0:T(128)} %param.13) | copy-start | bytes 388

commit v2 on v1

--- a/solution.py
+++ b/solution.py
@@ -87,7 +87,7 @@
 
 
 def inputs_and_outputs():
-    return ("x_hbm", "g_hbm", "raw", "bias", "rate", "skip", "b", "c",
+    return ("x_hbm", "g_hbm", "raw_hbm", "bias_hbm", "rate_hbm", "skip_hbm", "b_hbm", "c_hbm",
             "gx", "graw", "ztot", "grate", "gskip", "gbias")
 
 
@@ -99,6 +99,12 @@
     halves = (2, groups, GROUP, half, state)
     segments = (2, chunks, CHUNK, state)
     return dict(
+        raw=vmem((heads, tokens), F32),
+        bias=vmem((1, heads), F32),
+        rate=vmem((1, heads), F32),
+        skip=vmem((1, heads), F32),
+        b=vmem((tokens, state), BF16),
+        c=vmem((tokens, state), BF16),
         src=vmem((2, groups, tokens, wide), BF16),
         xt=vmem((groups, wide, tokens), BF16),
         gt=vmem((groups, wide, tokens), BF16),
@@ -117,6 +123,8 @@
         agg=vmem(halves, F32),
         chip_in=vmem((chips,) + halves[1:], F32),
         pre=vmem(halves, F32),
+        post=vmem(halves[1:], F32),
+        link=vmem((heads, CHUNK), F32),
         give=vmem(halves, F32),
         state_in=vmem((2, groups, GROUP, size, state), F32),
         dxt=vmem((groups, chunks, wide, CHUNK), F32),
@@ -129,6 +137,7 @@
         zsum=vmem(segments, F32),
         zin=vmem((2,) + segments, F32),
         params_in=vmem((peers, heads, CHUNK), F32),
+        small_sem=dma((6,)),
         load_sem=dma((2, groups)),
         end_send=dma((peers,)),
         end_recv=dma((peers,)),
@@ -160,6 +169,14 @@
     early = jnp.where(chip < chips // 2, 0, 1)
     late = 1 - early
 
+    tree = chips == 4
+    is_inner = jnp.logical_or(chip == 1, chip == 2)
+    is_outer = jnp.logical_not(is_inner)
+    inner_chip = jnp.where(chip < 2, 1, 2)
+    pair_place = me + 2 - 4 * (chip % 2)
+    across_place = me + 4 - 8 * (chip // 2)
+    forwarded = groups // 2
+
     left = zpos < line // 2
     inner = jnp.where(left, zpos + 1, zpos - 1)
     outer = jnp.where(left, zpos - 1, zpos + 1)
@@ -190,12 +207,24 @@
         at = pl.ds(pl.multiple_of(group * wide, wide), wide)
         return pltpu.make_async_copy((k.g_hbm, k.x_hbm)[e].at[:, at], k.src.at[e, group], k.load_sem.at[e, group])
 
-    def start_loads():
-        for group in range(groups):
+    def small_loads():
+        pairs = ((k.raw_hbm, k.raw), (k.bias_hbm, k.bias), (k.rate_hbm, k.rate), (k.skip_hbm, k.skip),
+                 (k.b_hbm, k.b), (k.c_hbm, k.c))
+        return [pltpu.make_async_copy(src, dst, k.small_sem.at[i]) for i, (src, dst) in enumerate(pairs)]
+
+    def start_small():
+        for copy in small_loads():
+            copy.start()
+
+    def start_loads(first, last):
+        for group in range(first, last):
             load(1, group).start()
             load(0, group).start()
 
     def prepare():
+        for copy in small_loads():
+            copy.wait()
+        start_loads(1, groups)
         dt = softplus(k.raw[...] + column_of(k.bias[...]))
         k.dt[...] = dt
         log_decay = -column_of(k.rate[...]) * dt
@@ -238,6 +267,93 @@
         return remote(k.agg.at[what, group], k.chip_in.at[step, group],
                       k.chip_send.at[step, group], k.chip_recv.at[step, group], ctx=(me + 2 * step) % peers)
 
+    def tree_copy(slot, group, source):
+        place = across_place if slot == 2 else pair_place
+        return remote(source, k.chip_in.at[slot, group],
+                      k.chip_send.at[slot, group], k.chip_recv.at[slot, group], ctx=place)
+
+    def tree_arrival(slot, group):
+        tree_copy(slot, group, k.post.at[group]).wait_recv()
+
+    def tree_exchange(group):
+        near = jnp.where(is_outer, early, late)
+        if group < forwarded:
+            tree_copy(1, group, k.agg.at[near, group]).start()
+            return
+
+        @pl.when(is_outer)
+        def _():
+            tree_copy(1, group, k.agg.at[early, group]).start()
+
+        @pl.when(is_inner)
+        def _():
+            tree_copy(3, group, k.agg.at[early, group]).start()
+            if group == groups - 1:
+                for other in range(forwarded, groups):
+                    tree_copy(1, other, k.agg.at[late, other]).start()
+
+    def hand(group):
+        link = k.link[rows_of(group)]
+
+        @pl.when(is_inner)
+        def _():
+            tree_arrival(1, group)
+            k.post[group] = k.agg[early, group] + scaled(link, k.chip_in[1, group])
+            tree_copy(2, group, k.post.at[group]).start()
+
+        if group >= forwarded:
+            @pl.when(is_outer)
+            def _():
+                tree_arrival(3, group)
+                k.post[group] = k.chip_in[3, group] + scaled(link, k.agg[early, group])
+                tree_copy(2, group, k.post.at[group]).start()
+
+    def forward(group):
+        @pl.when(is_outer)
+        def _():
+            tree_arrival(2, group)
+            tree_copy(3, group, k.chip_in.at[2, group]).start()
+
+    def tree_early(group):
+        @pl.when(is_inner)
+        def _():
+            k.pre[early, group] = k.chip_in[1, group]
+
+        @pl.when(is_outer)
+        def _():
+            k.pre[early, group] = jnp.zeros((GROUP, half, state), F32)
+
+        hand_back(early, group)
+
+    def tree_late(group):
+        @pl.when(is_inner)
+        def _():
+            slot = 3 if group < forwarded else 2
+            tree_arrival(slot, group)
+            k.pre[late, group] = k.chip_in[slot, group]
+
+        @pl.when(is_outer)
+        def _():
+            tree_arrival(1, group)
+            if group >= forwarded:
+                tree_arrival(2, group)
+            k.pre[late, group] = k.chip_in[1, group] + scaled(k.link[rows_of(group)], k.chip_in[2, group])
+
+        hand_back(late, group)
+
+    def tree_drain(group):
+        tree_copy(1, group, k.post.at[group]).wait_send()
+
+        @pl.when(is_inner)
+        def _():
+            tree_copy(2, group, k.post.at[group]).wait_send()
+            if group >= forwarded:
+                tree_copy(3, group, k.post.at[group]).wait_send()
+
+        @pl.when(is_outer)
+        def _():
+            tree_copy(3 if group < forwarded else 2, group, k.post.at[group]).wait_send()
+
     def back_copy(e, group, rows):
         return remote(k.give.at[e, group], k.state_in.at[e, group, :, rows, :],
                       k.back_send.at[e, group], k.back_recv.at[e, group], ctx=mate)
@@ -280,6 +396,8 @@
             high = (chip + step) % chips
             s_log = s_log + (k.ends[2 * low] + k.ends[2 * low + 1])
             r_log = r_log + (k.ends[2 * high] + k.ends[2 * high + 1])
+        if tree:
+            k.link[...] = jnp.exp(k.ends[2 * inner_chip] + k.ends[2 * inner_chip + 1])
 
     def scaled(coef, block):
         return coef[:, None, :] * block
@@ -293,8 +411,7 @@
         return own, jnp.exp(k.ends[mate, at_rows]), jnp.ones_like(own), jnp.zeros_like(own)
 
     def combine(group):
-        @pl.when(group == 0)
-        def _():
+        if group == 0:
             end_copy(mate_step, mate).wait_recv()
 
         own_e, mate_e, one, _ = own_and_mate(group)
@@ -304,7 +421,7 @@
             k.agg[e, group] = (scaled(jnp.where(down, one, mate_e), k.total[e, group, :, mine, :])
                                + scaled(jnp.where(down, own_e, one), k.pair_in[e, group]))
 
-    def finalize(e, group):
+    def gather(e, group):
         at_rows = rows_of(group)
         k.pre[e, group] = jnp.zeros((GROUP, half, state), F32)
         for step in range(1, chips):
@@ -315,6 +432,9 @@
                 chip_copy(slot, group).wait_recv()
                 k.pre[e, group] += scaled(k.coef[e, step, at_rows], k.chip_in[slot, group])
 
+        hand_back(e, group)
+
+    def hand_back(e, group):
         own_e, mate_e, one, zero = own_and_mate(group)
         down = downstream(e)
         pre = k.pre[e, group]
@@ -502,40 +622,43 @@
 
     def exchange(group):
         combine(group)
-        for n in range(1, min(3, chips)):
+        if tree:
+            tree_exchange(group)
+            return
+        for n in range(1, chips):
             chip_copy(nth_step(n), group).start()
 
-    def first_step(group, carry):
+    start_small()
+    start_loads(0, 1)
+    greet()
+    prepare()
+    met()
+    send_ends()
+    for group in range(groups):
         states(group)
         pair_copy(0, group).start()
         backs(group)
         pair_copy(1, group).start()
-
-        @pl.when(group > 0)
-        def _():
+        if group > 0:
             exchange(group - 1)
-
-        return carry
-
-    greet()
-    start_loads()
-    prepare()
-    met()
-    send_ends()
-    lax.fori_loop(0, groups, first_step, 0)
-
-    done = 0
     for group in range(groups):
         within(group)
         if group == 0:
             exchange(groups - 1)
-            for n in range(3, chips):
-                lax.fori_loop(0, groups, lambda group, carry: (chip_copy(nth_step(n), group).start(), carry)[1], 0)
             make_coefs()
-        if group >= 1 or groups == 1:
-            while done < min(group + 1, groups) and (group == groups - 1 or done < group):
-                finalize(early, done)
-                done += 1
+        if tree:
+            hand(group)
+            if 2 <= group < forwarded + 2:
+                forward(group - 2)
+            if group > 0:
+                tree_early(group - 1)
+    if tree:
+        for group in range(max(groups - 2, 0), forwarded):
+            forward(group)
+        tree_early(groups - 1)
+    else:
+        for group in range(groups):
+            gather(early, group)
     score_parts()
 
     pieces = [(e, c) for e in (early, late) for c in range(chunks)]
@@ -554,18 +677,17 @@
         projections(early, c)
         publish(early, c)
     for group in range(groups):
-        finalize(late, group)
-        tend(min(group, 3), 0)
+        (tree_late if tree else functools.partial(gather, late))(group)
+    tend(1, 0)
     for c in range(chunks):
         projections(late, c)
         publish(late, c)
-        tend(chunks, (1, 2, 3, 4)[min(c, 3)])
+        tend((2, 2, 3, 4)[min(c, 3)], (0, 0, 1, 2)[min(c, 3)])
     turns = [(c, group) for c in range(chunks) for group in range(groups)]
     for j, turn in enumerate(turns):
         inputs_step(*turn)
         part = 16 * (j + 1) // len(turns)
-        tend(chunks + sum(part >= at for at in (2, 6, 10, 13)), chunks + sum(part >= at for at in (10, 14)))
-    tend(len(pieces), 0)
+        tend(chunks + sum(part >= at for at in (3, 9, 16)), chunks - 2 + sum(part >= at for at in (5, 12, 16)))
     step_sizes()
     for d in range(1, peers):
         params_copy(d, me).start()
@@ -579,8 +701,11 @@
             for e in range(2):
                 pair_copy(e, group).wait_send()
                 back_copy(e, group, mine).wait_send()
-            for step in range(1, chips):
-                chip_copy(step, group).wait_send()
+            if tree:
+                tree_drain(group)
+            else:
+                for step in range(1, chips):
+                    chip_copy(step, group).wait_send()
         for c in range(chunks):
             for e in range(2):
                 inward(e, c, k.zsum).wait_send()
@@ -626,7 +751,7 @@
     row = shape(1, heads)
     results = pl.pallas_call(
         functools.partial(kernel, names, peers, line),
-        in_specs=[hbm, hbm] + [vmem] * 6,
+        in_specs=[pl.BlockSpec(memory_space=pltpu.HBM)] * 8,
         out_specs=[vmem] * 6,
         out_shape=[shape(groups, chunks, CHUNK, GROUP * size, dtype=BF16), shape(heads, tokens),
                    shape(2, chunks, CHUNK, state), row, row, row],
@@ -634,7 +759,8 @@
         compiler_params=pltpu.CompilerParams(
             collective_id=0, has_side_effects=True, vmem_limit_bytes=VMEM_LIMIT),
         name="layer",
-    )(tokens_x, grad_y, raw_dt, step_bias[None], decay_rate[None], skip_gain[None], in_b, in_c)
+    )(*[pltpu.with_memory_space_constraint(a, pltpu.HBM) for a in (
+        tokens_x, grad_y, raw_dt, step_bias[None], decay_rate[None], skip_gain[None], in_b, in_c)])
     gx, graw, gb, gc, grate, gskip, gbias = pl.pallas_call(
         functools.partial(finish_kernel, groups, chunks),
         in_specs=[vmem] * 6,

time: 57.9 us -> 48 us (0.83)
  Pallas kernels: 52.3 us -> 47 us
  local copies, waits for them, and re-layouts: 4.6 us -> 0 us
    pallas_call x1, Pallas kernels: 50.5 us -> 45.3 us  [on_device(): pl.pallas_call(functools.partial(kernel, names, peers, line), in_specs=[p...]
    unnamed x12 -> x0, local copies, waits for them, and re-layouts: 4.6 us -> none
where the time goes in v2:
time: 48 us; the launch traced here: 47.8 us
  Pallas kernels  47 us (98%)
  between operations  0.8 us (2%)
    pallas_call x1, Pallas kernels, on_device(): pl.pallas_call(functools.partial(kernel, names, peers, line), in_specs=[p...  45.3 us
    pallas_call x1, Pallas kernels, on_device(): pl.pallas_call(functools.partial(finish_kernel, groups, chunks), in_specs...  1.74 us

profile of v2, /device:TPU:0, one launch (start us, length us, event | category | flops | bytes accessed | tf_op | source)
XLA Modules:
  0.0 47.8 jit_solution(9713522822992820159)
XLA Ops:
  0.6 45.3 %layer.1 = (bf16[4,4,128,512]{3,2,1,0:T(8,128)(2,1)S(1)}, f32[32,512]{1,0:T(8,128)S(1)}, f32[2,4,128,128]{3,2,1,0:T(8,128)S(1)}, f32[1,32]{1,0:T(1,128)S(1)}, f32[1,32]{1,0:T(1,128)S(1)}, /*index=5*/f32[1,32]{1,0:T(1,128)S(1)}) custom-call(bf16[512,2048]{1,0:T(8,128)(2,1)} %refs_0_.1, bf16[512,2048]{1,0:T(8,128)(2,1)} %refs_1_.1, f32[32,512]{1,0:T(8,128)} %refs_2_.1, ...), custom_call_target="tpu_custom_call" | custom-call | tf_op jit(solution)/shard_map/layer/pallas_call | solution.py:752
  45.9 1.7 %finish.1 = (bf16[512,2048]{1,0:T(8,128)(2,1)}, f32[32,512]{1,0:T(8,128)}, f32[512,128]{1,0:T(8,128)}, f32[512,128]{1,0:T(8,128)}, f32[1,32]{1,0:T(1,128)}, /*index=5*/f32[1,32]{1,0:T(1,128)}, f32[1,32]{1,0:T(1,128)}) custom-call(bf16[4,4,128,512]{3,2,1,0:T(8,128)(2,1)S(1)} %get-tuple-element.20.gx, f32[32,512]{1,0:T(8,128)S(1)} %get-tuple-element.21.graw, ...), custom_call_target="tpu_custom_call" | custom-call | tf_op jit(solution)/shard_map/finish/pallas_call | solution.py:764

commit v3 on v2

--- a/solution.py
+++ b/solution.py
@@ -16,6 +16,8 @@
 NT = (((1,), (1,)), ((), ()))
 MESH = pl.DeviceIdType.MESH
 VMEM_LIMIT = 50 << 20
+LOG2_E = 1.4426950408889634
+HANDS = (0, 1, 1, 2)
 
 
 def mm(a, b):
@@ -118,6 +120,7 @@
         local=vmem((2, groups, chunks, wide, state), F32),
         total=vmem((2, groups, GROUP, size, state), F32),
         ends=vmem((peers, heads, CHUNK), F32),
+        end_rows=vmem((peers, 1, heads), F32),
         coef=vmem((2, chips, heads, CHUNK), F32),
         pair_in=vmem(halves, F32),
         agg=vmem(halves, F32),
@@ -139,19 +142,19 @@
         params_in=vmem((peers, heads, CHUNK), F32),
         small_sem=dma((6,)),
         load_sem=dma((2, groups)),
-        end_send=dma((peers,)),
-        end_recv=dma((peers,)),
-        pair_send=dma((2, groups)),
+        end_send=dma(()),
+        end_recv=dma((2,)),
+        pair_send=dma(()),
         pair_recv=dma((2, groups)),
-        chip_send=dma((chips, groups)),
-        chip_recv=dma((chips, groups)),
-        back_send=dma((2, groups)),
+        chip_send=dma((chips,)),
+        chip_recv=dma((chips - 1, groups)),
+        back_send=dma(()),
         back_recv=dma((2, groups)),
-        in_send=dma((2, chunks)),
-        out_send=dma((2, chunks)),
+        in_send=dma(()),
+        out_send=dma(()),
         z_recv=dma((2, 2, chunks)),
-        param_send=dma((peers,)),
-        param_recv=dma((peers,)),
+        param_send=dma(()),
+        param_recv=dma(()),
     )
 
 
@@ -166,6 +169,7 @@
     me, zpos = lax.axis_index("ctx"), lax.axis_index("head")
     odd, chip = me % 2, me // 2
     mate = me + 1 - 2 * odd
+    mate_step = jnp.where(odd == 1, 1, peers - 1)
     early = jnp.where(chip < chips // 2, 0, 1)
     late = 1 - early
 
@@ -239,6 +243,7 @@
             after = after + ends[chunks - 1 - c]
         k.whole[...] = jnp.exp(before)
         k.ends[me] = before
+        k.end_rows[me] = row_of(before[:, 0:1])
         for c in range(chunks):
             k.cum[:, span_of(c)] = cums[c]
             k.scale[0, :, span_of(c)] = jnp.exp(cums[c])
@@ -248,8 +253,13 @@
         k.skips[...] = lanes(column_of(k.skip[...]))
 
     def end_copy(d, place):
-        return remote(k.ends.at[place], k.ends.at[place], k.end_send.at[d], k.end_recv.at[d],
+        slot = jnp.where(d == peers - mate_step, 1, 0)
+        return remote(k.end_rows.at[place], k.end_rows.at[place], k.end_send, k.end_recv.at[slot],
                       ctx=(me + d) % peers)
+
+    def end_arrival(slot, count):
+        some = k.end_rows.at[pl.ds(0, count)]
+        remote(some, some, k.end_send, k.end_recv.at[slot], ctx=mate).wait_recv()
 
     def send_ends():
         for d in range(1, peers):
@@ -260,17 +270,17 @@
 
     def pair_copy(e, group):
         return remote(k.total.at[e, group, :, theirs, :], k.pair_in.at[e, group],
-                      k.pair_send.at[e, group], k.pair_recv.at[e, group], ctx=mate)
+                      k.pair_send, k.pair_recv.at[e, group], ctx=mate)
 
     def chip_copy(step, group):
         what = jnp.where(chip + step < chips, 0, 1)
         return remote(k.agg.at[what, group], k.chip_in.at[step, group],
-                      k.chip_send.at[step, group], k.chip_recv.at[step, group], ctx=(me + 2 * step) % peers)
+                      k.chip_send.at[step], k.chip_recv.at[step - 1, group], ctx=(me + 2 * step) % peers)
 
     def tree_copy(slot, group, source):
         place = across_place if slot == 2 else pair_place
         return remote(source, k.chip_in.at[slot, group],
-                      k.chip_send.at[slot, group], k.chip_recv.at[slot, group], ctx=place)
+                      k.chip_send.at[slot], k.chip_recv.at[slot - 1, group], ctx=place)
 
     def tree_arrival(slot, group):
         tree_copy(slot, group, k.post.at[group]).wait_recv()
@@ -341,22 +351,29 @@
 
         hand_back(late, group)
 
-    def tree_drain(group):
-        tree_copy(1, group, k.post.at[group]).wait_send()
+    def sent(slot, count):
+        some = k.chip_in.at[slot, pl.ds(0, count)]
+        remote(some, some, k.chip_send.at[slot], k.chip_recv.at[slot - 1, 0], ctx=mate).wait_send()
+
+    def tree_drain():
+        sent(1, groups)
 
         @pl.when(is_inner)
         def _():
-            tree_copy(2, group, k.post.at[group]).wait_send()
-            if group >= forwarded:
-                tree_copy(3, group, k.post.at[group]).wait_send()
+            sent(2, groups)
+            if forwarded < groups:
+                sent(3, groups - forwarded)
 
         @pl.when(is_outer)
         def _():
-            tree_copy(3 if group < forwarded else 2, group, k.post.at[group]).wait_send()
+            if forwarded < groups:
+                sent(2, groups - forwarded)
+            if forwarded:
+                sent(3, forwarded)
 
     def back_copy(e, group, rows):
         return remote(k.give.at[e, group], k.state_in.at[e, group, :, rows, :],
-                      k.back_send.at[e, group], k.back_recv.at[e, group], ctx=mate)
+                      k.back_send, k.back_recv.at[e, group], ctx=mate)
 
     def rows_of(group):
         return pl.ds(pl.multiple_of(group * GROUP, GROUP), GROUP)
@@ -383,10 +400,10 @@
         carry_local(1, group, reversed(range(chunks)), k.gt, k.c)
 
     def make_coefs():
-        for d in range(1, peers):
-            @pl.when(d != mate_step)
-            def _():
-                end_copy(d, (me - d + peers) % peers).wait_recv()
+        if peers > 2:
+            end_arrival(0, peers - 2)
+            for d in range(peers):
+                k.ends[d] = lanes(column_of(k.end_rows[d]))
         s_log = jnp.zeros((heads, CHUNK), F32)
         r_log = jnp.zeros((heads, CHUNK), F32)
         for step in range(1, chips):
@@ -412,7 +429,8 @@
 
     def combine(group):
         if group == 0:
-            end_copy(mate_step, mate).wait_recv()
+            end_arrival(1, 1)
+            k.ends[mate] = lanes(column_of(k.end_rows[mate]))
 
         own_e, mate_e, one, _ = own_and_mate(group)
         for e in range(2):
@@ -447,12 +465,13 @@
     causal = triangle(False)
 
     def within(group):
-        def one_chunk(c, carry):
-            at = pl.ds(pl.multiple_of(c * CHUNK, CHUNK), CHUNK)
+        for c in range(chunks):
+            at = span_of(c)
             scores = mm_nt(k.b[at, :], k.c[at, :])
-            cum = k.cum[rows_of(group), at]
-            shifted = (cum - jnp.log(k.dt[rows_of(group), at])).T
-            total = jnp.zeros((CHUNK, CHUNK), F32)
+            dt = k.dt[rows_of(group), at]
+            cum = k.cum[rows_of(group), at] * LOG2_E
+            shifted = (cum - jnp.log2(dt)).T
+            total = k.dg[c]
             rows, cols = [], []
             for pair in range(GROUP // 2):
                 x_pair = k.src[1, group, at, pair * 2 * size:(pair + 1) * 2 * size]
@@ -461,7 +480,7 @@
                 for j in range(2):
                     h = 2 * pair + j
                     gap = cum[h:h + 1, :] - shifted[:, h:h + 1]
-                    decay = jnp.exp(jnp.where(causal, gap, -1e30))
+                    decay = jnp.exp2(jnp.where(causal, gap, -1e30))
                     both = products[:, j * CHUNK:(j + 1) * CHUNK] * decay
                     total = total + both
                     rows.append(jnp.sum(both * scores, axis=0, keepdims=True))
@@ -472,10 +491,7 @@
                     cols.append(jnp.sum(dx_h * x_h.astype(F32), axis=0, keepdims=True))
             k.row[group, c] = jnp.concatenate(rows, axis=0)
             k.col[group, c] = jnp.concatenate(cols, axis=0)
-            k.dg[c] += total
-            return carry
-
-        lax.fori_loop(0, chunks, one_chunk, 0)
+            k.dg[c] = total
 
     def score_parts():
         for c in range(chunks):
@@ -484,10 +500,10 @@
                 high, low = split(dg)
                 k.zown[e, c] = mm(jnp.concatenate([high, low], axis=1), twice(operand[at, :], 0))
 
-    def projections(e, c):
+    def projections(e, c, members):
         at = span_of(c)
         total = k.zown[e, c]
-        for group in range(groups):
+        for group in members:
             if c == 0:
                 back_copy(e, group, theirs).wait_recv()
             at_rows = rows_of(group)
@@ -510,11 +526,11 @@
 
     def inward(e, c, source):
         return remote(source.at[e, c], k.zin.at[in_slot, e, c],
-                      k.in_send.at[e, c], k.z_recv.at[in_slot, e, c], head=inner)
+                      k.in_send, k.z_recv.at[in_slot, e, c], head=inner)
 
     def outward(e, c, slot=1):
         return remote(k.ztot.at[e, c], k.zin.at[slot, e, c],
-                      k.out_send.at[e, c], k.z_recv.at[slot, e, c], head=outer)
+                      k.out_send, k.z_recv.at[slot, e, c], head=outer)
 
     def publish(e, c):
         @pl.when(jnp.logical_not(has_outer))
@@ -602,20 +618,21 @@
         k.params_in[me] = jnp.where(lane == 0, g_rate, jnp.where(lane == 1, g_skip, g_bias))
 
     def params_copy(d, place):
-        return remote(k.params_in.at[place], k.params_in.at[place], k.param_send.at[d], k.param_recv.at[d],
+        return remote(k.params_in.at[place], k.params_in.at[place], k.param_send, k.param_recv,
                       ctx=(me + d) % peers)
 
+    def every_param():
+        some = k.params_in.at[pl.ds(0, peers - 1)]
+        return remote(some, some, k.param_send, k.param_recv, ctx=mate)
+
     def gather_params():
-        for d in range(1, peers):
-            params_copy(d, (me - d + peers) % peers).wait_recv()
+        every_param().wait_recv()
         total = k.params_in[0]
         for d in range(1, peers):
             total = total + k.params_in[d]
         k.grate[...] = row_of(total[:, 0:1])
         k.gskip[...] = row_of(total[:, 1:2])
         k.gbias[...] = row_of(total[:, 2:3])
-
-    mate_step = jnp.where(odd == 1, 1, peers - 1)
 
     def nth_step(n):
         return jnp.where(chip < chips // 2, n, chips - n)
@@ -641,26 +658,6 @@
         pair_copy(1, group).start()
         if group > 0:
             exchange(group - 1)
-    for group in range(groups):
-        within(group)
-        if group == 0:
-            exchange(groups - 1)
-            make_coefs()
-        if tree:
-            hand(group)
-            if 2 <= group < forwarded + 2:
-                forward(group - 2)
-            if group > 0:
-                tree_early(group - 1)
-    if tree:
-        for group in range(max(groups - 2, 0), forwarded):
-            forward(group)
-        tree_early(groups - 1)
-    else:
-        for group in range(groups):
-            gather(early, group)
-    score_parts()
-
     pieces = [(e, c) for e in (early, late) for c in range(chunks)]
     relayed, settled = 0, 0
 
@@ -673,21 +670,78 @@
             settle_mid(*pieces[settled])
             settled += 1
 
-    for c in range(chunks):
-        projections(early, c)
-        publish(early, c)
-    for group in range(groups):
-        (tree_late if tree else functools.partial(gather, late))(group)
-    tend(1, 0)
-    for c in range(chunks):
-        projections(late, c)
-        publish(late, c)
-        tend((2, 2, 3, 4)[min(c, 3)], (0, 0, 1, 2)[min(c, 3)])
-    turns = [(c, group) for c in range(chunks) for group in range(groups)]
+    everyone = list(range(groups))
+    if tree:
+        handed, returned, passed = 0, 0, 0
+
+        def pass_on(hands, returns, forwards):
+            nonlocal handed, returned, passed
+            while handed < min(hands, groups):
+                hand(handed)
+                handed += 1
+            while returned < min(returns, groups):
+                tree_early(returned)
+                returned += 1
+            while passed < min(forwards, forwarded):
+                forward(passed)
+                passed += 1
+
+        for group in everyone:
+            within(group)
+            if group == 0:
+                exchange(groups - 1)
+                make_coefs()
+            pass_on(HANDS[min(group, 3)], HANDS[min(group, 3)], 0)
+        score_parts()
+        first = everyone[:groups - 2]
+        pass_on(groups - 2, groups - 2, 0)
+        for c in range(chunks):
+            projections(early, c, first)
+            if c == chunks // 2 - 1:
+                pass_on(groups - 1, groups - 1, 1)
+        pass_on(groups, groups, 1)
+        sooner = everyone[0::2][:groups - 1]
+        later = [group for group in everyone if group not in sooner]
+        for c in range(chunks):
+            if c == chunks - 1:
+                for group in sooner:
+                    tree_late(group)
+            projections(early, c, everyone[len(first):])
+            publish(early, c)
+            if c == 0:
+                pass_on(groups, groups, groups)
+        for c in range(chunks):
+            projections(late, c, sooner)
+            if c == chunks // 2 - 1:
+                for group in later:
+                    tree_late(group)
+                tend(1, 0)
+        tend(2, 0)
+        for c in range(chunks):
+            projections(late, c, later)
+            publish(late, c)
+            tend((3, 3, 4, 4)[min(c, 3)], (0, 0, 0, 1)[min(c, 3)])
+    else:
+        for group in everyone:
+            within(group)
+            if group == 0:
+                exchange(groups - 1)
+                make_coefs()
+        score_parts()
+        for e in (early, late):
+            for group in everyone:
+                gather(e, group)
+            for c in range(chunks):
+                projections(e, c, everyone)
+                publish(e, c)
+        tend(chunks, 1)
+    turns = [(c, group) for c in range(chunks) for group in everyone]
     for j, turn in enumerate(turns):
         inputs_step(*turn)
         part = 16 * (j + 1) // len(turns)
-        tend(chunks + sum(part >= at for at in (3, 9, 16)), chunks - 2 + sum(part >= at for at in (5, 12, 16)))
+        for n, at in enumerate((2, 6, 10, 15)):
+            if part >= at:
+                tend(chunks + 1 + n, chunks - 2 + n)
     step_sizes()
     for d in range(1, peers):
         params_copy(d, me).start()
@@ -697,25 +751,22 @@
     gather_params()
 
     def drain():
-        for group in range(groups):
-            for e in range(2):
-                pair_copy(e, group).wait_send()
-                back_copy(e, group, mine).wait_send()
-            if tree:
-                tree_drain(group)
-            else:
-                for step in range(1, chips):
-                    chip_copy(step, group).wait_send()
-        for c in range(chunks):
-            for e in range(2):
-                inward(e, c, k.zsum).wait_send()
-
-                @pl.when(has_outer)
-                def _():
-                    outward(e, c).wait_send()
-        for d in range(1, peers):
-            end_copy(d, me).wait_send()
-            params_copy(d, me).wait_send()
+        remote(k.pair_in, k.pair_in, k.pair_send, k.pair_recv.at[0, 0], ctx=mate).wait_send()
+        remote(k.give, k.give, k.back_send, k.back_recv.at[0, 0], ctx=mate).wait_send()
+        if tree:
+            tree_drain()
+        else:
+            for step in range(1, chips):
+                sent(step, groups)
+        remote(k.zown, k.zown, k.in_send, k.z_recv.at[0, 0, 0], head=inner).wait_send()
+
+        @pl.when(has_outer)
+        def _():
+            remote(k.zown, k.zown, k.out_send, k.z_recv.at[0, 0, 0], head=outer).wait_send()
+
+        some = k.end_rows.at[pl.ds(0, peers - 1)]
+        remote(some, some, k.end_send, k.end_recv.at[0], ctx=mate).wait_send()
+        every_param().wait_send()
 
     drain()
 

time: 48 us -> 46.4 us (0.967)
  Pallas kernels: 47 us -> 45.4 us
    pallas_call x1, Pallas kernels: 45.3 us -> 43.7 us  [on_device(): pl.pallas_call(functools.partial(kernel, names, peers, line), in_specs=[p...]
where the time goes in v3:
time: 46.4 us; the launch traced here: 46.2 us
  Pallas kernels  45.4 us (98%)
  between operations  0.8 us (2%)
    pallas_call x1, Pallas kernels, on_device(): pl.pallas_call(functools.partial(kernel, names, peers, line), in_specs=[p...  43.7 us
    pallas_call x1, Pallas kernels, on_device(): pl.pallas_call(functools.partial(finish_kernel, groups, chunks), in_specs...  1.74 us

profile of v3, /device:TPU:0, one launch (start us, length us, event | category | flops | bytes accessed | tf_op | source)
XLA Modules:
  0.0 46.2 jit_solution(4140251942598528214)
XLA Ops:
  0.6 43.7 %layer.1 = (bf16[4,4,128,512]{3,2,1,0:T(8,128)(2,1)S(1)}, f32[32,512]{1,0:T(8,128)S(1)}, f32[2,4,128,128]{3,2,1,0:T(8,128)S(1)}, f32[1,32]{1,0:T(1,128)S(1)}, f32[1,32]{1,0:T(1,128)S(1)}, /*index=5*/f32[1,32]{1,0:T(1,128)S(1)}) custom-call(bf16[512,2048]{1,0:T(8,128)(2,1)} %refs_0_.1, bf16[512,2048]{1,0:T(8,128)(2,1)} %refs_1_.1, f32[32,512]{1,0:T(8,128)} %refs_2_.1, ...), custom_call_target="tpu_custom_call" | custom-call | tf_op jit(solution)/shard_map/layer/pallas_call | solution.py:803
  44.3 1.7 %finish.1 = (bf16[512,2048]{1,0:T(8,128)(2,1)}, f32[32,512]{1,0:T(8,128)}, f32[512,128]{1,0:T(8,128)}, f32[512,128]{1,0:T(8,128)}, f32[1,32]{1,0:T(1,128)}, /*index=5*/f32[1,32]{1,0:T(1,128)}, f32[1,32]{1,0:T(1,128)}) custom-call(bf16[4,4,128,512]{3,2,1,0:T(8,128)(2,1)S(1)} %get-tuple-element.20.gx, f32[32,512]{1,0:T(8,128)S(1)} %get-tuple-element.21.graw, ...), custom_call_target="tpu_custom_call" | custom-call | tf_op jit(solution)/shard_map/finish/pallas_call | solution.py:815

commit v4 on v3

--- a/solution.py
+++ b/solution.py
@@ -17,7 +17,8 @@
 MESH = pl.DeviceIdType.MESH
 VMEM_LIMIT = 50 << 20
 LOG2_E = 1.4426950408889634
-HANDS = (0, 1, 1, 2)
+HANDS = (1, 1, 2, 2)
+LATE_TURNS = ((1, 0, 1), (2, 1, 1), (4, 2, 2), (6, 3, 2), (8, 4, 2), (9, 4, 3), (10, 5, 3), (12, 6, 3), (13, 6, 4), (14, 7, 4), (16, 8, 5))
 
 
 def mm(a, b):
@@ -99,7 +100,7 @@
     vmem = pltpu.VMEM
     dma = pltpu.SemaphoreType.DMA
     halves = (2, groups, GROUP, half, state)
-    segments = (2, chunks, CHUNK, state)
+    segments = (2, tokens, state)
     return dict(
         raw=vmem((heads, tokens), F32),
         bias=vmem((1, heads), F32),
@@ -152,7 +153,7 @@
         back_recv=dma((2, groups)),
         in_send=dma(()),
         out_send=dma(()),
-        z_recv=dma((2, 2, chunks)),
+        z_recv=dma((2, 3 * chunks)),
         param_send=dma(()),
         param_recv=dma(()),
     )
@@ -249,8 +250,6 @@
             k.scale[0, :, span_of(c)] = jnp.exp(cums[c])
             k.scale[1, :, span_of(c)] = jnp.exp(ends[c] - cums[c]) * dt[:, span_of(c)]
             k.step[c] = jnp.exp(ends[c])
-        k.dg[...] = jnp.zeros_like(k.dg)
-        k.skips[...] = lanes(column_of(k.skip[...]))
 
     def end_copy(d, place):
         slot = jnp.where(d == peers - mate_step, 1, 0)
@@ -427,17 +426,17 @@
         own = jnp.exp(k.ends[me, at_rows])
         return own, jnp.exp(k.ends[mate, at_rows]), jnp.ones_like(own), jnp.zeros_like(own)
 
-    def combine(group):
-        if group == 0:
-            end_arrival(1, 1)
-            k.ends[mate] = lanes(column_of(k.end_rows[mate]))
-
+    def learn_mate():
+        end_arrival(1, 1)
+        k.ends[mate] = lanes(column_of(k.end_rows[mate]))
+        k.skips[...] = lanes(column_of(k.skip[...]))
+
+    def combine(e, group):
         own_e, mate_e, one, _ = own_and_mate(group)
-        for e in range(2):
-            down = downstream(e)
-            pair_copy(e, group).wait_recv()
-            k.agg[e, group] = (scaled(jnp.where(down, one, mate_e), k.total[e, group, :, mine, :])
-                               + scaled(jnp.where(down, own_e, one), k.pair_in[e, group]))
+        down = downstream(e)
+        pair_copy(e, group).wait_recv()
+        k.agg[e, group] = (scaled(jnp.where(down, one, mate_e), k.total[e, group, :, mine, :])
+                           + scaled(jnp.where(down, own_e, one), k.pair_in[e, group]))
 
     def gather(e, group):
         at_rows = rows_of(group)
@@ -471,7 +470,7 @@
             dt = k.dt[rows_of(group), at]
             cum = k.cum[rows_of(group), at] * LOG2_E
             shifted = (cum - jnp.log2(dt)).T
-            total = k.dg[c]
+            total = k.dg[c] if group else jnp.zeros((CHUNK, CHUNK), F32)
             rows, cols = [], []
             for pair in range(GROUP // 2):
                 x_pair = k.src[1, group, at, pair * 2 * size:(pair + 1) * 2 * size]
@@ -498,11 +497,11 @@
             at = span_of(c)
             for e, dg, operand in ((0, k.dg[c].T, k.b), (1, k.dg[c], k.c)):
                 high, low = split(dg)
-                k.zown[e, c] = mm(jnp.concatenate([high, low], axis=1), twice(operand[at, :], 0))
+                k.zown[e, at] = mm(jnp.concatenate([high, low], axis=1), twice(operand[at, :], 0))
 
     def projections(e, c, members):
         at = span_of(c)
-        total = k.zown[e, c]
+        total = k.zown[e, at]
         for group in members:
             if c == 0:
                 back_copy(e, group, theirs).wait_recv()
@@ -522,56 +521,63 @@
                 for j in range(2):
                     h = 2 * pair + j
                     total = total + both[:, j * state:(j + 1) * state] * column[:, h:h + 1]
-        k.zown[e, c] = total
-
-    def inward(e, c, source):
-        return remote(source.at[e, c], k.zin.at[in_slot, e, c],
-                      k.in_send, k.z_recv.at[in_slot, e, c], head=inner)
-
-    def outward(e, c, slot=1):
-        return remote(k.ztot.at[e, c], k.zin.at[slot, e, c],
-                      k.out_send, k.z_recv.at[slot, e, c], head=outer)
-
-    def publish(e, c):
+        k.zown[e, at] = total
+
+    pieces = [(early, slice(c * CHUNK, (c + 1) * CHUNK)) for c in range(chunks)]
+    pieces += [(late, slice(r * (CHUNK // 2), (r + 1) * (CHUNK // 2))) for r in range(2 * chunks)]
+
+    def inward(n, source):
+        e, at = pieces[n]
+        return remote(source.at[e, at], k.zin.at[in_slot, e, at], k.in_send, k.z_recv.at[in_slot, n], head=inner)
+
+    def outward(n, slot=1):
+        e, at = pieces[n]
+        return remote(k.ztot.at[e, at], k.zin.at[slot, e, at], k.out_send, k.z_recv.at[slot, n], head=outer)
+
+    def publish(first, last):
         @pl.when(jnp.logical_not(has_outer))
         def _():
-            inward(e, c, k.zown).start()
-
-    def relay(e, c):
+            for n in range(first, last):
+                inward(n, k.zown).start()
+
+    def relay(n):
+        e, at = pieces[n]
+
         @pl.when(has_outer)
         def _():
-            outward(e, c, 0).wait_recv()
-            k.zsum[e, c] = k.zown[e, c] + k.zin[0, e, c]
-            inward(e, c, k.zsum).start()
-
-    def settle(e, c):
-        outward(e, c).wait_recv()
+            outward(n, 0).wait_recv()
+            k.zsum[e, at] = k.zown[e, at] + k.zin[0, e, at]
+            inward(n, k.zsum).start()
+
+    def settle(n):
+        e, at = pieces[n]
+        outward(n).wait_recv()
 
         @pl.when(jnp.logical_and(is_mid, has_outer))
         def _():
-            k.ztot[e, c] = k.zsum[e, c] + k.zin[1, e, c]
+            k.ztot[e, at] = k.zsum[e, at] + k.zin[1, e, at]
 
         @pl.when(jnp.logical_and(is_mid, jnp.logical_not(has_outer)))
         def _():
-            k.ztot[e, c] = k.zown[e, c] + k.zin[1, e, c]
+            k.ztot[e, at] = k.zown[e, at] + k.zin[1, e, at]
 
         @pl.when(jnp.logical_not(is_mid))
         def _():
-            k.ztot[e, c] = k.zin[1, e, c]
+            k.ztot[e, at] = k.zin[1, e, at]
 
         @pl.when(has_outer)
         def _():
-            outward(e, c).start()
-
-    def settle_mid(e, c):
+            outward(n).start()
+
+    def settle_mid(n):
         @pl.when(is_mid)
         def _():
-            settle(e, c)
-
-    def settle_rest(e, c):
+            settle(n)
+
+    def settle_rest(n):
         @pl.when(jnp.logical_not(is_mid))
         def _():
-            settle(e, c)
+            settle(n)
 
     def inputs_step(c, group):
         at, at_rows = span_of(c), rows_of(group)
@@ -586,7 +592,7 @@
         product = head_sums(xt * gt, GROUP)
         k.cross[group] = product if c == 0 else k.cross[group] + product
         dx = dx + k.dxt[group, c] + per_head(k.skips[at_rows], gt)
-        k.gx[group, c] = dx.astype(BF16).T
+        k.gx[group, at] = dx.astype(BF16).T
 
     def step_sizes():
         rate, bias = column_of(k.rate[...]), column_of(k.bias[...])
@@ -638,7 +644,9 @@
         return jnp.where(chip < chips // 2, n, chips - n)
 
     def exchange(group):
-        combine(group)
+        if group:
+            combine(0, group)
+            combine(1, group)
         if tree:
             tree_exchange(group)
             return
@@ -651,23 +659,50 @@
     prepare()
     met()
     send_ends()
-    for group in range(groups):
+    def forth(group):
         states(group)
         pair_copy(0, group).start()
+
+    def back(group):
         backs(group)
         pair_copy(1, group).start()
-        if group > 0:
+
+    @pl.when(chip % 2 == 0)
+    def _():
+        forth(0)
+        back(0)
+
+    @pl.when(chip % 2 == 1)
+    def _():
+        back(0)
+        forth(0)
+
+    learn_mate()
+    forerunner = chip % 2
+    combine(forerunner, 0)
+    if tree and forwarded:
+        exchange(0)
+    for group in range(1, groups):
+        forth(group)
+        if group == 1:
+            combine(1 - forerunner, 0)
+            if not tree:
+                exchange(0)
+        back(group)
+        if group > 1:
             exchange(group - 1)
-    pieces = [(e, c) for e in (early, late) for c in range(chunks)]
+    if groups == 1:
+        combine(1 - forerunner, 0)
+
     relayed, settled = 0, 0
 
     def tend(relays, settles):
         nonlocal relayed, settled
         while relayed < min(relays, len(pieces)):
-            relay(*pieces[relayed])
+            relay(relayed)
             relayed += 1
         while settled < min(settles, relayed):
-            settle_mid(*pieces[settled])
+            settle_mid(settled)
             settled += 1
 
     everyone = list(range(groups))
@@ -694,12 +729,10 @@
             pass_on(HANDS[min(group, 3)], HANDS[min(group, 3)], 0)
         score_parts()
         first = everyone[:groups - 2]
-        pass_on(groups - 2, groups - 2, 0)
+        pass_on(groups - 1, groups - 1, 1)
         for c in range(chunks):
             projections(early, c, first)
-            if c == chunks // 2 - 1:
-                pass_on(groups - 1, groups - 1, 1)
-        pass_on(groups, groups, 1)
+        pass_on(groups, groups, groups)
         sooner = everyone[0::2][:groups - 1]
         later = [group for group in everyone if group not in sooner]
         for c in range(chunks):
@@ -707,20 +740,20 @@
                 for group in sooner:
                     tree_late(group)
             projections(early, c, everyone[len(first):])
-            publish(early, c)
+            publish(c, c + 1)
             if c == 0:
                 pass_on(groups, groups, groups)
         for c in range(chunks):
             projections(late, c, sooner)
             if c == chunks // 2 - 1:
+                tend(1, 0)
                 for group in later:
                     tree_late(group)
-                tend(1, 0)
-        tend(2, 0)
+            tend(max(0, c - 1), 0)
         for c in range(chunks):
             projections(late, c, later)
-            publish(late, c)
-            tend((3, 3, 4, 4)[min(c, 3)], (0, 0, 0, 1)[min(c, 3)])
+            publish(chunks + 2 * c, chunks + 2 * c + 2)
+            tend((3, 3, 3, 4)[min(c, 3)], 0)
     else:
         for group in everyone:
             within(group)
@@ -733,21 +766,21 @@
                 gather(e, group)
             for c in range(chunks):
                 projections(e, c, everyone)
-                publish(e, c)
+        publish(0, len(pieces))
         tend(chunks, 1)
     turns = [(c, group) for c in range(chunks) for group in everyone]
     for j, turn in enumerate(turns):
         inputs_step(*turn)
         part = 16 * (j + 1) // len(turns)
-        for n, at in enumerate((2, 6, 10, 15)):
+        for at, relays, settles in LATE_TURNS:
             if part >= at:
-                tend(chunks + 1 + n, chunks - 2 + n)
+                tend(chunks + relays, settles)
     step_sizes()
     for d in range(1, peers):
         params_copy(d, me).start()
     tend(len(pieces), len(pieces))
-    for piece in pieces:
-        settle_rest(*piece)
+    for n in range(len(pieces)):
+        settle_rest(n)
     gather_params()
 
     def drain():
@@ -758,11 +791,11 @@
         else:
             for step in range(1, chips):
                 sent(step, groups)
-        remote(k.zown, k.zown, k.in_send, k.z_recv.at[0, 0, 0], head=inner).wait_send()
+        remote(k.zown, k.zown, k.in_send, k.z_recv.at[0, 0], head=inner).wait_send()
 
         @pl.when(has_outer)
         def _():
-            remote(k.zown, k.zown, k.out_send, k.z_recv.at[0, 0, 0], head=outer).wait_send()
+            remote(k.zown, k.zown, k.out_send, k.z_recv.at[0, 0], head=outer).wait_send()
 
         some = k.end_rows.at[pl.ds(0, peers - 1)]
         remote(some, some, k.end_send, k.end_recv.at[0], ctx=mate).wait_send()
@@ -771,14 +804,11 @@
     drain()
 
 
-def finish_kernel(groups, chunks, gx, graw, ztot, grate, gskip, gbias,
+def finish_kernel(groups, gx, graw, ztot, grate, gskip, gbias,
                   gx_out, graw_out, gb_out, gc_out, grate_out, gskip_out, gbias_out, sems):
-    wide = gx.shape[3]
-    copies = [(gx.at[group, c], gx_out.at[span_of(c), group * wide:(group + 1) * wide])
-              for group in range(groups) for c in range(chunks)]
-    copies += [(ztot.at[1 - i, c], ref.at[span_of(c), :]) for i, ref in enumerate((gb_out, gc_out))
-               for c in range(chunks)]
-    copies += [(graw, graw_out), (grate, grate_out), (gskip, gskip_out), (gbias, gbias_out)]
+    wide = gx.shape[2]
+    copies = [(gx.at[group], gx_out.at[:, group * wide:(group + 1) * wide]) for group in range(groups)]
+    copies += [(ztot.at[1], gb_out), (ztot.at[0], gc_out), (graw, graw_out), (grate, grate_out), (gskip, gskip_out), (gbias, gbias_out)]
     copies = [pltpu.make_async_copy(src, dst, sems.at[i]) for i, (src, dst) in enumerate(copies)]
     for copy in copies:
         copy.start()
@@ -791,7 +821,7 @@
     width = tokens_x.shape[1]
     size = width // heads
     state = in_b.shape[1]
-    groups, chunks = heads // GROUP, tokens // CHUNK
+    groups = heads // GROUP
     scratch = scratch_of(heads, tokens, size, state, peers)
     names = inputs_and_outputs() + tuple(scratch)
 
@@ -804,8 +834,8 @@
         functools.partial(kernel, names, peers, line),
         in_specs=[pl.BlockSpec(memory_space=pltpu.HBM)] * 8,
         out_specs=[vmem] * 6,
-        out_shape=[shape(groups, chunks, CHUNK, GROUP * size, dtype=BF16), shape(heads, tokens),
-                   shape(2, chunks, CHUNK, state), row, row, row],
+        out_shape=[shape(groups, tokens, GROUP * size, dtype=BF16), shape(heads, tokens),
+                   shape(2, tokens, state), row, row, row],
         scratch_shapes=list(scratch.values()),
         compiler_params=pltpu.CompilerParams(
             collective_id=0, has_side_effects=True, vmem_limit_bytes=VMEM_LIMIT),
@@ -813,12 +843,12 @@
     )(*[pltpu.with_memory_space_constraint(a, pltpu.HBM) for a in (
         tokens_x, grad_y, raw_dt, step_bias[None], decay_rate[None], skip_gain[None], in_b, in_c)])
     gx, graw, gb, gc, grate, gskip, gbias = pl.pallas_call(
-        functools.partial(finish_kernel, groups, chunks),
+        functools.partial(finish_kernel, groups),
         in_specs=[vmem] * 6,
         out_specs=[hbm] * 7,
         out_shape=[shape(tokens, width, dtype=BF16), shape(heads, tokens), shape(tokens, state),
                    shape(tokens, state), row, row, row],
-        scratch_shapes=[pltpu.SemaphoreType.DMA((groups * chunks + 2 * chunks + 4,))],
+        scratch_shapes=[pltpu.SemaphoreType.DMA((groups + 6,))],
         compiler_params=pltpu.CompilerParams(vmem_limit_bytes=4 << 20),
         name="finish",
     )(*results)

time: 46.4 us -> 45.6 us (0.983)
  Pallas kernels: 45.4 us -> 44.6 us
    pallas_call x1, Pallas kernels: 43.7 us -> 43 us  [on_device(): pl.pallas_call(functools.partial(kernel, names, peers, line), in_specs=[p...]
where the time goes in v4:
time: 45.6 us; the launch traced here: 45.4 us
  Pallas kernels  44.6 us (98%)
  between operations  0.8 us (2%)
    pallas_call x1, Pallas kernels, on_device(): pl.pallas_call(functools.partial(kernel, names, peers, line), in_specs=[p...  43 us
    pallas_call x1, Pallas kernels, on_device(): pl.pallas_call(functools.partial(finish_kernel, groups), in_specs=[vmem]...  1.59 us

profile of v4, /device:TPU:0, one launch (start us, length us, event | category | flops | bytes accessed | tf_op | source)
XLA Modules:
  0.0 45.4 jit_solution(16147178841916892446)
XLA Ops:
  0.6 43.0 %layer.1 = (bf16[4,512,512]{2,1,0:T(8,128)(2,1)S(1)}, f32[32,512]{1,0:T(8,128)S(1)}, f32[2,512,128]{2,1,0:T(8,128)S(1)}, f32[1,32]{1,0:T(1,128)S(1)}, f32[1,32]{1,0:T(1,128)S(1)}, /*index=5*/f32[1,32]{1,0:T(1,128)S(1)}) custom-call(bf16[512,2048]{1,0:T(8,128)(2,1)} %refs_0_.1, bf16[512,2048]{1,0:T(8,128)(2,1)} %refs_1_.1, f32[32,512]{1,0:T(8,128)} %refs_2_.1, ...), custom_call_target="tpu_custom_call" | custom-call | tf_op jit(solution)/shard_map/layer/pallas_call | solution.py:833
  43.7 1.6 %finish.1 = (bf16[512,2048]{1,0:T(8,128)(2,1)}, f32[32,512]{1,0:T(8,128)}, f32[512,128]{1,0:T(8,128)}, f32[512,128]{1,0:T(8,128)}, f32[1,32]{1,0:T(1,128)}, /*index=5*/f32[1,32]{1,0:T(1,128)}, f32[1,32]{1,0:T(1,128)}) custom-call(bf16[4,512,512]{2,1,0:T(8,128)(2,1)S(1)} %get-tuple-element.20.gx, f32[32,512]{1,0:T(8,128)S(1)} %get-tuple-element.21.graw, ...), custom_call_target="tpu_custom_call" | custom-call | tf_op jit(solution)/shard_map/finish/pallas_call | solution.py:845

commit v5 on v4

--- a/solution.py
+++ b/solution.py
@@ -213,13 +213,17 @@
         return pltpu.make_async_copy((k.g_hbm, k.x_hbm)[e].at[:, at], k.src.at[e, group], k.load_sem.at[e, group])
 
     def small_loads():
-        pairs = ((k.raw_hbm, k.raw), (k.bias_hbm, k.bias), (k.rate_hbm, k.rate), (k.skip_hbm, k.skip),
-                 (k.b_hbm, k.b), (k.c_hbm, k.c))
+        pairs = ((k.raw_hbm, k.raw), (k.bias_hbm, k.bias), (k.rate_hbm, k.rate),
+                 (k.b_hbm, k.b), (k.c_hbm, k.c), (k.skip_hbm, k.skip))
         return [pltpu.make_async_copy(src, dst, k.small_sem.at[i]) for i, (src, dst) in enumerate(pairs)]
 
-    def start_small():
-        for copy in small_loads():
+    def start_small(first, last):
+        for copy in small_loads()[first:last]:
             copy.start()
+
+    def wait_small(first, last):
+        for copy in small_loads()[first:last]:
+            copy.wait()
 
     def start_loads(first, last):
         for group in range(first, last):
@@ -227,14 +231,15 @@
             load(0, group).start()
 
     def prepare():
-        for copy in small_loads():
-            copy.wait()
+        wait_small(0, 3)
         start_loads(1, groups)
         dt = softplus(k.raw[...] + column_of(k.bias[...]))
         k.dt[...] = dt
         log_decay = -column_of(k.rate[...]) * dt
         ones = triangle(False).astype(F32)
-        cums = [jnp.dot(log_decay[:, span_of(c)], ones, precision=HIGH) for c in range(chunks)]
+        stacked = jnp.concatenate([log_decay[:, span_of(c)] for c in range(chunks)], axis=0)
+        stacked = jnp.dot(stacked, ones, precision=HIGH)
+        cums = [stacked[c * heads:(c + 1) * heads] for c in range(chunks)]
         ends = [lanes(cum[:, CHUNK - 1:]) for cum in cums]
         before, after = jnp.zeros_like(ends[0]), jnp.zeros_like(ends[0])
         for c in range(chunks):
@@ -653,12 +658,12 @@
         for n in range(1, chips):
             chip_copy(nth_step(n), group).start()
 
-    start_small()
+    start_small(0, 3)
     start_loads(0, 1)
+    start_small(3, 6)
     greet()
     prepare()
-    met()
-    send_ends()
+    wait_small(3, 6)
     def forth(group):
         states(group)
         pair_copy(0, group).start()
@@ -667,18 +672,30 @@
         backs(group)
         pair_copy(1, group).start()
 
-    @pl.when(chip % 2 == 0)
+    forerunner = chip % 2
+
+    @pl.when(forerunner == 0)
     def _():
-        forth(0)
-        back(0)
-
-    @pl.when(chip % 2 == 1)
+        states(0)
+
+    @pl.when(forerunner == 1)
     def _():
-        back(0)
-        forth(0)
-
+        backs(0)
+
+    met()
+    pair_copy(forerunner, 0).start()
+    send_ends()
+
+    @pl.when(forerunner == 0)
+    def _():
+        backs(0)
+
+    @pl.when(forerunner == 1)
+    def _():
+        states(0)
+
+    pair_copy(1 - forerunner, 0).start()
     learn_mate()
-    forerunner = chip % 2
     combine(forerunner, 0)
     if tree and forwarded:
         exchange(0)

time: 45.6 us -> 45.2 us (level)
  no operation moved by 1% of the time
where the time goes in v5:
time: 45.2 us; the launch traced here: 45.1 us
  Pallas kernels  44.3 us (98%)
  between operations  0.8 us (2%)
    pallas_call x1, Pallas kernels, on_device(): pl.pallas_call(functools.partial(kernel, names, peers, line), in_specs=[p...  42.7 us
    pallas_call x1, Pallas kernels, on_device(): pl.pallas_call(functools.partial(finish_kernel, groups), in_specs=[vmem]...  1.59 us

profile of v5, /device:TPU:0, one launch (start us, length us, event | category | flops | bytes accessed | tf_op | source)
XLA Modules:
  0.0 45.1 jit_solution(87727719338213819)
XLA Ops:
  0.6 42.7 %layer.1 = (bf16[4,512,512]{2,1,0:T(8,128)(2,1)S(1)}, f32[32,512]{1,0:T(8,128)S(1)}, f32[2,512,128]{2,1,0:T(8,128)S(1)}, f32[1,32]{1,0:T(1,128)S(1)}, f32[1,32]{1,0:T(1,128)S(1)}, /*index=5*/f32[1,32]{1,0:T(1,128)S(1)}) custom-call(bf16[512,2048]{1,0:T(8,128)(2,1)} %refs_0_.1, bf16[512,2048]{1,0:T(8,128)(2,1)} %refs_1_.1, f32[32,512]{1,0:T(8,128)} %refs_2_.1, ...), custom_call_target="tpu_custom_call" | custom-call | tf_op jit(solution)/shard_map/layer/pallas_call | solution.py:850
  43.3 1.6 %finish.1 = (bf16[512,2048]{1,0:T(8,128)(2,1)}, f32[32,512]{1,0:T(8,128)}, f32[512,128]{1,0:T(8,128)}, f32[512,128]{1,0:T(8,128)}, f32[1,32]{1,0:T(1,128)}, /*index=5*/f32[1,32]{1,0:T(1,128)}, f32[1,32]{1,0:T(1,128)}) custom-call(bf16[4,512,512]{2,1,0:T(8,128)(2,1)S(1)} %get-tuple-element.20.gx, f32[32,512]{1,0:T(8,128)S(1)} %get-tuple-element.21.graw, ...), custom_call_target="tpu_custom_call" | custom-call | tf_op jit(solution)/shard_map/finish/pallas_call | solution.py:862

commit v6 on v5

--- a/solution.py
+++ b/solution.py
@@ -468,8 +468,8 @@
 
     causal = triangle(False)
 
-    def within(group):
-        for c in range(chunks):
+    def within(group, first=0, last=chunks):
+        for c in range(first, last):
             at = span_of(c)
             scores = mm_nt(k.b[at, :], k.c[at, :])
             dt = k.dt[rows_of(group), at]
@@ -739,7 +739,12 @@
                 passed += 1
 
         for group in everyone:
-            within(group)
+            if group == 2:
+                within(group, 0, chunks - 1)
+                pass_on(2, 1, 0)
+                within(group, chunks - 1)
+            else:
+                within(group)
             if group == 0:
                 exchange(groups - 1)
                 make_coefs()
@@ -749,6 +754,7 @@
         pass_on(groups - 1, groups - 1, 1)
         for c in range(chunks):
             projections(early, c, first)
+        pass_on(groups - 1, groups - 1, groups)
         pass_on(groups, groups, groups)
         sooner = everyone[0::2][:groups - 1]
         later = [group for group in everyone if group not in sooner]

time: 45.2 us -> 45.2 us (level)
  no operation moved by 1% of the time
where the time goes in v6:
time: 45.2 us; the launch traced here: 45.1 us
  Pallas kernels  44.3 us (98%)
  between operations  0.8 us (2%)
    pallas_call x1, Pallas kernels, on_device(): pl.pallas_call(functools.partial(kernel, names, peers, line), in_specs=[p...  42.7 us
    pallas_call x1, Pallas kernels, on_device(): pl.pallas_call(functools.partial(finish_kernel, groups), in_specs=[vmem]...  1.59 us

profile of v6, /device:TPU:0, one launch (start us, length us, event | category | flops | bytes accessed | tf_op | source)
XLA Modules:
  0.0 45.1 jit_solution(7683194235772273095)
XLA Ops:
  0.6 42.7 %layer.1 = (bf16[4,512,512]{2,1,0:T(8,128)(2,1)S(1)}, f32[32,512]{1,0:T(8,128)S(1)}, f32[2,512,128]{2,1,0:T(8,128)S(1)}, f32[1,32]{1,0:T(1,128)S(1)}, f32[1,32]{1,0:T(1,128)S(1)}, /*index=5*/f32[1,32]{1,0:T(1,128)S(1)}) custom-call(bf16[512,2048]{1,0:T(8,128)(2,1)} %refs_0_.1, bf16[512,2048]{1,0:T(8,128)(2,1)} %refs_1_.1, f32[32,512]{1,0:T(8,128)} %refs_2_.1, ...), custom_call_target="tpu_custom_call" | custom-call | tf_op jit(solution)/shard_map/layer/pallas_call | solution.py:856
  43.3 1.6 %finish.1 = (bf16[512,2048]{1,0:T(8,128)(2,1)}, f32[32,512]{1,0:T(8,128)}, f32[512,128]{1,0:T(8,128)}, f32[512,128]{1,0:T(8,128)}, f32[1,32]{1,0:T(1,128)}, /*index=5*/f32[1,32]{1,0:T(1,128)}, f32[1,32]{1,0:T(1,128)}) custom-call(bf16[4,512,512]{2,1,0:T(8,128)(2,1)S(1)} %get-tuple-element.20.gx, f32[32,512]{1,0:T(8,128)S(1)} %get-tuple-element.21.graw, ...), custom_call_target="tpu_custom_call" | custom-call | tf_op jit(solution)/shard_map/finish/pallas_call | solution.py:868
